TPU v7x, 32 devices: a whole 2x2x4 slice. The times are simulated.
32 devices in a mesh: space: 8 (over z, y), mem: 4 (over x, core).
Axes of the slice: x: 2, y: 2, z: 4, core: 2. Of those that a mesh axis runs over, the one named last changes fastest.
Arguments:
- prior_ensemble: float32 [512, 32, 128], P('mem', 'space'), may hold values from -70 to 70
- stencil_factors: float32 [4, 32, 128], P(None, 'space'), may hold values from 0.02 to 0.22
- sea_mask: int32 [32, 128], P('space'), may hold values 0 or 1
- measured_site_positions: int32 [8, 128], P('space'), may hold values from 0 to 511
- measured_data: float32 [1024], P('space'), may hold values from -16 to 16
- measurement_precision: float32 [1024], P('space'), may hold values from 0.5 to 2
- cotangent: float32 [512, 32, 128], P('mem', 'space'), may hold values from -6 to 6
Outputs:
- grad_prior: float32 [512, 32, 128], P('mem', 'space')
- grad_coef: float32 [4, 32, 128], P(None, 'space')
Inputs may be any that keep to these rules, and one draw needn't show every extreme that they name: `measured_site_positions`: the flat position row * 128 + column, within its strip of 4 rows, of each observed cell; strip s holds rows s * 4 to (s + 1) * 4 - 1. `sea_mask`: 1 marks a sea cell, 0 a land cell.
All inputs are finite; a program needn't handle non-finite values. No bound on the sum of `sea_mask` on one device may be relied on, other than what follows from the above.
Results may differ from a plain program's by a relative error of at most 0.0003.
Values sent between devices are 32-bit elements; how exact they have to be, the bound alone decides.
A program may use at most 64 MiB of HBM per device.

v0:
```python
import functools
import jax
import jax.numpy as jnp
from jax import lax
from jax.experimental import pallas as pl
from jax.experimental.pallas import tpu as pltpu
from jax.sharding import PartitionSpec as P

MESH = pl.DeviceIdType.MESH
F32 = jnp.float32
BF16 = jnp.bfloat16
VMEM_SPEC = pl.BlockSpec(memory_space=pltpu.VMEM)


def remote(src, dst, send, recv, s, m):
    return pltpu.make_async_remote_copy(
        src_ref=src, dst_ref=dst, send_sem=send, recv_sem=recv, device_id=(s, m), device_id_type=MESH
    )


def split(x):
    lead = x.astype(BF16)
    return lead, (x - lead.astype(F32)).astype(BF16)


def split3(x):
    lead = x.astype(BF16)
    rest = x - lead.astype(F32)
    middle = rest.astype(BF16)
    return lead, middle, (rest - middle.astype(F32)).astype(BF16)


def plain(a, b):
    return jnp.dot(a, b, preferred_element_type=F32)


def plain_t(a, b):
    return lax.dot_general(a, b, (((1,), (1,)), ((), ())), preferred_element_type=F32)


def mm3(a, b):
    return plain(a[0], b[0]) + (plain(a[0], b[1]) + plain(a[1], b[0]))


def mm3_t(a, b):
    return plain_t(a[0], b[0]) + (plain_t(a[0], b[1]) + plain_t(a[1], b[0]))


def whole_sum(x):
    return jnp.sum(jnp.sum(x, axis=0, keepdims=True), axis=1, keepdims=True)


def eye(size):
    return lax.broadcasted_iota(jnp.int32, (size, size), 0) == lax.broadcasted_iota(
        jnp.int32, (size, size), 1
    )


class Sizes:
    def __init__(self, n_space, n_mem, prior, sites):
        self.n_space, self.n_mem = n_space, n_mem
        self.members, self.rows, self.cols = prior.shape
        self.total = self.members * n_mem
        self.sites = sites.shape[-1]
        self.height = self.members // n_space
        self.near = 2 if n_space % 2 == 0 else 1
        self.far = n_space // self.near
        self.half = 2 if n_mem % 2 == 0 else 1
        self.wide = n_mem // self.half
        self.group = max(1, self.far // 4)
        self.groups = self.far // self.group


def scratch_of(z):
    dma = pltpu.SemaphoreType.DMA
    ext = z.rows + 4
    v = lambda *shape: pltpu.VMEM(shape, F32)
    b = lambda *shape: pltpu.VMEM(shape, BF16)
    square = (z.total, z.total)
    return dict(
        pext=v(ext, z.members, z.cols),
        aux=v(ext, 8, z.cols),
        cotf=v(z.rows, z.total, z.cols),
        chi=b(z.rows, z.total, z.cols),
        clo=b(z.rows, z.total, z.cols),
        fext=v(z.rows + 2, z.members, z.cols),
        state=v(z.rows, z.members, z.cols),
        hot=b(z.rows, z.cols, z.sites),
        obsf=v(z.total, z.sites),
        tanh=v(z.members, z.sites),
        anom=v(z.total, z.sites),
        innov=v(8, z.sites),
        sums=v(z.n_mem, 8 * pl.cdiv(z.rows, 8), z.cols),
        dmat=v(z.n_mem, z.members, z.members),
        dx=v(z.n_mem, z.members, z.members),
        rsrc=v(z.n_space, z.height, z.total),
        rbuf=v(z.n_space, z.height, z.total),
        vec=v(8, z.members),
        vbuf=v(z.n_space, 8, z.members),
        vout=v(z.n_mem, 8, z.members),
        out=v(z.n_mem, z.far, z.near, z.height, z.total),
        f=v(*square),
        f2=v(*square),
        t=v(*square),
        s=v(*square),
        u=v(*square),
        y=v(*square),
        vcol=v(z.total, 8),
        sbext=v(ext, z.members, z.cols),
        fbar=v(z.rows + 2, z.members, z.cols),
        cbuf=v(z.n_mem, 4 * z.rows, z.cols),
        own=dma((2, z.rows)),
        keep=dma((2,)),
        halo=dma((2, 2)),
        aux_halo=dma((2, 2)),
        bar_halo=dma((2, 2)),
        cot_sem=dma((2, z.half, z.wide)),
        obs_sem=dma((2, z.half, z.wide)),
        sum_sem=dma((2, z.n_mem)),
        d_sem=dma((2, z.n_mem)),
        rs_sem=dma((2, z.n_space)),
        v_sem=dma((2, z.n_space)),
        vg_sem=dma((2, z.n_mem)),
        c_sem=dma((2, z.n_mem)),
        a_sem=dma((2, z.far)),
        b_sem=dma((2, z.near, z.groups)),
        p_sem=dma((2, z.wide, z.near, z.groups)),
        q_sem=dma((2, z.half, z.wide, z.near, z.groups)),
    )


class Step:
    def __init__(self, z, refs):
        self.z = z
        self.__dict__.update(refs)
        self.s_id, self.m_id = lax.axis_index("space"), lax.axis_index("mem")
        self.waits = []

    def finish_sends(self):
        for copy, when in self.waits:
            if when is None:
                copy.wait_send()
            else:
                pl.when(when)(copy.wait_send)

    def barrier(self):
        z, s, m = self.z, self.s_id, self.m_id
        peers = [(lax.rem(s + k, z.n_space), m) for k in range(1, z.n_space)]
        peers += [(s, lax.rem(m + k, z.n_mem)) for k in range(1, z.n_mem)]
        barrier = pltpu.get_barrier_semaphore()
        for peer in peers:
            pl.semaphore_signal(barrier, inc=1, device_id=peer, device_id_type=MESH)
        return lambda: pl.semaphore_wait(barrier, len(peers))

    def halo_send(self, ref, sem):
        z, s, m = self.z, self.s_id, self.m_id
        has_low, has_high = s > 0, s < z.n_space - 1
        r = z.rows
        up = remote(ref.at[pl.ds(r, 2)], ref.at[pl.ds(0, 2)], sem.at[0, 0], sem.at[1, 0], s + 1, m)
        down = remote(
            ref.at[pl.ds(2, 2)], ref.at[pl.ds(r + 2, 2)], sem.at[0, 1], sem.at[1, 1], s - 1, m
        )
        pl.when(has_high)(up.start)
        pl.when(has_low)(down.start)
        self.waits += [(up, has_high), (down, has_low)]

        def wait():
            pl.when(has_low)(up.wait_recv)
            pl.when(has_high)(down.wait_recv)

        return wait

    def pair_gather(self, part, sem):
        z, s, m = self.z, self.s_id, self.m_id
        p, q = m // z.half, lax.rem(m, z.half)
        across = [lax.rem(p + k, z.wide) * z.half + q for k in range(1, z.wide)]
        beside = [p * z.half + lax.rem(q + k, z.half) for k in range(1, z.half)]
        mine = part(m)
        hops, sides = [], []
        for k, to in enumerate(across):
            hops.append(remote(mine, mine, sem.at[0, 0, k + 1], sem.at[1, 0, k + 1], s, to))
            hops[-1].start()
        for k, to in enumerate(beside):
            sides.append(remote(mine, mine, sem.at[0, k + 1, 0], sem.at[1, k + 1, 0], s, to))
            sides[-1].start()

        def forward():
            for kp, hop in enumerate(hops):
                hop.wait_recv()
                piece = part(lax.rem(p + z.wide - kp - 1, z.wide) * z.half + q)
                for k, to in enumerate(beside):
                    copy = remote(
                        piece, piece, sem.at[0, k + 1, kp + 1], sem.at[1, k + 1, kp + 1], s, to
                    )
                    copy.start()
                    sides.append(copy)

        def wait():
            for copy in sides:
                copy.wait_recv()
            self.waits.extend((copy, None) for copy in hops + sides)

        return forward, wait

    def mem_send(self, ref, sem):
        z, s, m = self.z, self.s_id, self.m_id
        copies = []
        for k in range(1, z.n_mem):
            to = lax.rem(m + k, z.n_mem)
            copies.append(remote(ref.at[m], ref.at[m], sem.at[0, k], sem.at[1, k], s, to))
            copies[-1].start()

        def wait():
            for copy in copies:
                copy.wait_recv()
            self.waits.extend((copy, None) for copy in copies)

        return wait


    def coefficients(self, e):
        z = self.z
        c = [self.aux[e, k : k + 1, :] for k in range(4)]
        sea = self.aux[e, 4:5, :]
        lane = lax.broadcasted_iota(jnp.int32, (1, z.cols), 1)
        keep = sea * (1.0 - c[0] - c[1] - c[2] - c[3])
        west = jnp.where(lane == 0, 0.0, c[2])
        east = jnp.where(lane == z.cols - 1, 0.0, c[3])
        return keep, sea * c[0], sea * c[1], sea * west, sea * east

    def chunks(self):
        size = min(32, self.z.members)
        return [pl.ds(k, size) for k in range(0, self.z.members, size)]

    def advance(self, src, first, dst, count):
        z = self.z
        for i in range(count):
            keep, north, south, west, east = self.coefficients(first + i)
            for part in self.chunks():
                v = src[i + 1, part, :]
                dst[i, part, :] = (
                    keep * v
                    + north * src[i, part, :]
                    + south * src[i + 2, part, :]
                    + west * pltpu.roll(v, 1, 1)
                    + east * pltpu.roll(v, z.cols - 1, 1)
                )

    def observe(self):
        z = self.z
        picked = jnp.zeros((z.members, z.sites), F32)
        for r in range(z.rows):
            for piece in split3(self.state[r]):
                picked = picked + plain(piece, self.hot[r])
        tanh = jnp.tanh(picked)
        self.tanh[...] = tanh
        return picked + 0.5 * tanh

    def mark_sites(self):
        z = self.z
        for r in range(z.rows):
            cell = lax.broadcasted_iota(jnp.int32, (z.cols, z.sites), 0) + r * z.cols
            self.hot[r] = jnp.where(cell == self.sites[...], 1.0, 0.0).astype(BF16)


    def reduce_scatter(self):
        z, s, m = self.z, self.s_id, self.m_id
        copies = []
        for k in range(1, z.n_space):
            to = lax.rem(s + k, z.n_space)
            copies.append(
                remote(self.rsrc.at[to], self.rbuf.at[s], self.rs_sem.at[0, k], self.rs_sem.at[1, k], to, m)
            )
            copies[-1].start()
        tiny = []
        for k in range(1, z.n_space):
            to = lax.rem(s + k, z.n_space)
            tiny.append(remote(self.vec, self.vbuf.at[s], self.v_sem.at[0, k], self.v_sem.at[1, k], to, m))
            tiny[-1].start()
        self.rbuf[s] = self.rsrc[s]
        self.vbuf[s] = self.vec[...]
        for copy in copies:
            copy.wait_recv()
        total = self.rbuf[0]
        for k in range(1, z.n_space):
            total = total + self.rbuf[k]
        self.out[m, s // z.near, lax.rem(s, z.near)] = total
        self.waits += [(copy, None) for copy in copies + tiny]

        def small():
            for copy in tiny:
                copy.wait_recv()
            vec = self.vbuf[0]
            for k in range(1, z.n_space):
                vec = vec + self.vbuf[k]
            self.vout[m] = vec
            return self.mem_send(self.vout, self.vg_sem)

        return small

    def flow(self, which_b, start, index, kb, beside_b):
        z, s, m = self.z, self.s_id, self.m_id
        p, q = m // z.half, lax.rem(m, z.half)
        piece = self.out.at[m, pl.ds(start, z.group), which_b]
        to_send = []
        for kp in range(1, z.wide):
            to_send.append((
                self.p_sem.at[0, kp, kb, index], self.p_sem.at[1, kp, kb, index],
                s, lax.rem(p + kp, z.wide) * z.half + q,
            ))
        if beside_b:
            for k in range(1, z.near):
                to = (s // z.near) * z.near + lax.rem(which_b + k, z.near)
                to_send.append((self.b_sem.at[0, k, index], self.b_sem.at[1, k, index], to, m))
        for kq in range(1, z.half):
            to_send.append((
                self.q_sem.at[0, kq, 0, kb, index], self.q_sem.at[1, kq, 0, kb, index],
                s, p * z.half + lax.rem(q + kq, z.half),
            ))
        for item in to_send:
            copy = remote(piece, piece, *item)
            copy.start()
            self.waits.append((copy, None))

    def all_gather(self, small):
        z, s, m = self.z, self.s_id, self.m_id
        a, b = s // z.near, lax.rem(s, z.near)
        p, q = m // z.half, lax.rem(m, z.half)
        out = self.out
        stage_a = []
        for k in range(1, z.far):
            to = lax.rem(a + k, z.far)
            copy = remote(
                out.at[m, a, b], out.at[m, a, b], self.a_sem.at[0, k], self.a_sem.at[1, k],
                to * z.near + b, m,
            )
            copy.start()
            stage_a.append(copy)
        if z.group == 1:
            a_steps = [([], a)] + [
                ([stage_a[k - 1]], lax.rem(a + z.far - k, z.far)) for k in range(1, z.far)
            ]
        else:
            a_steps = [(stage_a if g == 0 else [], g * z.group) for g in range(z.groups)]
        steps_b = []
        small_wait = None
        for index, (needs, start) in enumerate(a_steps):
            for copy in needs:
                copy.wait_recv()
            steps_b.append((start, index))
            self.flow(b, start, index, 0, True)
            if index == 0:
                small_wait = small()
        self.waits += [(copy, None) for copy in stage_a]
        for start, index in steps_b:
            for kb in range(1, z.near):
                from_b = lax.rem(b + z.near - kb, z.near)
                piece = out.at[m, pl.ds(start, z.group), from_b]
                remote(
                    piece, piece, self.b_sem.at[0, kb, index], self.b_sem.at[1, kb, index], s, m
                ).wait_recv()
                self.flow(from_b, start, index, kb, False)
        for start, index in steps_b:
            for kb in range(z.near):
                which_b = lax.rem(b + z.near - kb, z.near)
                for kp in range(1, z.wide):
                    from_p = lax.rem(p + z.wide - kp, z.wide)
                    piece = out.at[from_p * z.half + q, pl.ds(start, z.group), which_b]
                    remote(
                        piece, piece, self.p_sem.at[0, kp, kb, index], self.p_sem.at[1, kp, kb, index], s, m
                    ).wait_recv()
                    for kq in range(1, z.half):
                        copy = remote(
                            piece, piece,
                            self.q_sem.at[0, kq, kp, kb, index], self.q_sem.at[1, kq, kp, kb, index],
                            s, p * z.half + lax.rem(q + kq, z.half),
                        )
                        copy.start()
                        self.waits.append((copy, None))
        for start, index in steps_b:
            for kb in range(z.near):
                which_b = lax.rem(b + z.near - kb, z.near)
                for kp in range(z.wide):
                    from_p = lax.rem(p + z.wide - kp, z.wide)
                    for kq in range(1, z.half):
                        from_q = lax.rem(q + z.half - kq, z.half)
                        piece = out.at[from_p * z.half + from_q, pl.ds(start, z.group), which_b]
                        remote(
                            piece, piece,
                            self.q_sem.at[0, kq, kp, kb, index], self.q_sem.at[1, kq, kp, kb, index], s, m,
                        ).wait_recv()
        small_wait()


    def holds_gram(self, k):
        n = self.z.n_mem
        if 2 * k < n:
            return True
        if 2 * k > n:
            return False
        return None

    def pack(self, scale):
        z, m = self.z, self.m_id
        lane8 = lax.broadcasted_iota(jnp.int32, (z.members, z.members), 1)
        mean = jnp.zeros((1, z.sites), F32)
        for k in range(z.n_mem):
            mean = mean + jnp.sum(self.obsf[k * z.members : (k + 1) * z.members, :], axis=0, keepdims=True)
        mean = mean / z.total
        prec = self.prec[...]
        innov = prec * (self.data[...] - mean)
        self.innov[0:1, :] = innov
        self.anom[...] = (self.obsf[...] - mean) * (prec / scale)
        blocks = [pl.ds(pl.multiple_of(lax.rem(m + k, z.n_mem) * z.members, z.members), z.members) for k in range(z.n_mem)]
        mine = self.anom[blocks[0], :]
        mine_split = split(mine)
        pull = jnp.sum(mine * innov, axis=1, keepdims=True)
        total = self.sums[0]
        for k in range(1, z.n_mem):
            total = total + self.sums[k]
        lacks = [
            (self.sums[k] / z.members - total / z.total) / scale for k in range(z.n_mem)
        ]
        terms = []
        lead = [jnp.concatenate([lacks[k][r : r + 1] for k in range(z.n_mem)] + [jnp.zeros((-z.n_mem % 8, z.cols), F32)] * (z.n_mem % 8 > 0), axis=0) for r in range(z.rows)]
        for r in range(z.rows):
            a = split(lead[r])
            b = (self.chi[r], self.clo[r])
            terms.append(mm3_t(a, b))
        term = terms[0]
        for other in terms[1:]:
            term = term + other
        self.corr[...] = term
        mean_bar = jnp.zeros((z.members, 1), F32)
        diagonal = eye(z.members)
        upper = lax.broadcasted_iota(jnp.int32, (z.members, z.members), 0) <= lane8
        for k in range(z.n_mem):
            b = blocks[k]
            cross = self.dmat[k] + self.pick_row(m, b)
            mean_bar = mean_bar + jnp.sum(cross, axis=1, keepdims=True)
            kind = self.holds_gram(k)
            gram = mm3_t(mine_split, split(self.anom[b, :])) if (k == 0 or kind is not False) else None
            if k == 0:
                sym = 0.5 * (cross + cross.T)
                own = jnp.sum(jnp.where(diagonal, sym, 0.0), axis=1, keepdims=True)
                block = jnp.where(upper, gram, sym)
            elif kind is True:
                block = gram
            else:
                there = lax.rem(m + k, z.n_mem)
                other = self.dx[k] + self.pick_row(there, blocks[0])
                block = 0.5 * (cross + other.T)
                if kind is None:
                    block = jnp.where(m < z.n_mem // 2, gram, block)
            self.rsrc[:, :, b] = block.reshape(z.n_space, z.height, z.members)
        lane = lax.broadcasted_iota(jnp.int32, (z.members, z.members), 1)
        columns = jnp.where(lane == 0, pull, jnp.where(lane == 1, mean_bar, jnp.where(lane == 2, own, 0.0)))
        self.vec[...] = columns.T[:8]

    def pick_row(self, which, cols):
        z = self.z
        rows = lax.broadcasted_iota(jnp.int32, (self.corr.shape[0], z.members), 0)
        return jnp.sum(jnp.where(rows == which, self.corr[:, cols], 0.0), axis=0, keepdims=True)

    def unpack(self, system, cross):
        z = self.z
        n = z.n_mem
        col = lambda k: slice(k * z.members, (k + 1) * z.members)
        lower = lax.broadcasted_iota(jnp.int32, (z.members, z.members), 0) > lax.broadcasted_iota(
            jnp.int32, (z.members, z.members), 1
        )
        diagonal = eye(z.members)
        read = lambda i, j: self.out[i, :, :, :, col(j)].reshape(z.members, z.members)
        for i in range(n):
            block = read(i, i)
            turned = block.T
            system[col(i), col(i)] = jnp.where(lower, turned, block) + diagonal.astype(F32)
            sym = jnp.where(lower, block, turned)
            cross[col(i), col(i)] = jnp.where(diagonal, self.vout[i, 2:3, :], sym)
            for j in range(i + 1, n):
                one, two = read(i, j), read(j, i)
                k = j - i
                gram_first = self.holds_gram(k)
                if gram_first is None:
                    gram_first = i < n // 2
                gram, sym = (one, two.T) if gram_first else (two.T, one)
                system[col(i), col(j)] = gram
                system[col(j), col(i)] = gram.T
                cross[col(i), col(j)] = sym
                cross[col(j), col(i)] = sym.T


    def analyse(self, scale):
        z, m = self.z, self.m_id
        total = z.total
        f_ref, f2_ref, t_ref, s_ref, u_ref, y_ref = self.f, self.f2, self.t, self.s, self.u, self.y
        offset = pl.multiple_of(m * z.members, z.members)
        mine = pl.ds(offset, z.members)
        self.unpack(f_ref, s_ref)
        identity = eye(total).astype(F32)
        norm = jnp.sqrt(whole_sum(f_ref[...] * f_ref[...]))
        root = jnp.sqrt(norm)
        f_ref[...] = 1.5 * identity - (0.5 / norm) * f_ref[...]
        f_split = split(f_ref[...])
        f2_ref[...] = mm3(f_split, f_split)
        f2_split = split(f2_ref[...])
        t_ref[...] = (1.5 * f_ref[...] + mm3(f2_split, split(f2_ref[...] - 1.5 * f_ref[...]))) / root
        t_split = split(t_ref[...])
        rows = jnp.concatenate([self.vout[k] for k in range(z.n_mem)], axis=1)
        rows = jnp.where(lax.broadcasted_iota(jnp.int32, rows.shape, 0) == 3, 1.0, rows)
        first = mm3(split(rows), t_split)
        second = mm3(split(first), t_split)
        turn = lambda x: x.T
        rows_t, first_t = turn(rows), turn(first)
        self.vcol[...] = turn(second)
        pull, mean_bar = rows[0:1], rows[1:2]
        weight = scale * s_ref[...] + 0.5 * (
            rows_t[:, 1:2] * first[0:1]
            + first_t[:, 0:1] * mean_bar
            + first_t[:, 1:2] * pull
            + rows_t[:, 0:1] * first[1:2]
        )
        scale_bar = -0.5 * whole_sum(weight * t_ref[...]) / norm
        s_ref[...] = weight / root
        s_split = split(s_ref[...])
        u_ref[...] = mm3(s_split, f2_split)
        y_ref[...] = mm3(s_split, split(2.0 * f2_ref[...] - 1.5 * f_ref[...]))
        y_ref[...] = 0.5 * (y_ref[...] + y_ref[...].T)
        approach = 1.5 * s_ref[...] - 1.5 * u_ref[...]
        approach = whole_sum(
            approach * (3.0 * identity - 2.0 * f_ref[...])
            + 2.0 * y_ref[...] * (3.0 * f_ref[...] - 2.0 * f2_ref[...])
        )
        scale_bar = scale_bar + 0.5 * approach / norm

        centred = lambda ref: ref[mine, :] - jnp.sum(ref[...], axis=0, keepdims=True) / total
        f_mine = centred(f_ref)
        bar = 1.5 * centred(s_ref) - 0.75 * (centred(u_ref) + mm3(split(centred(f2_ref)), s_split))
        bar = bar + mm3(split(centred(y_ref)), f_split) + mm3(split(f_mine), split(y_ref[...]))
        unit = (
            lax.broadcasted_iota(jnp.int32, (z.members, total), 0) + offset
            == lax.broadcasted_iota(jnp.int32, (z.members, total), 1)
        ).astype(F32) - 1.0 / total
        system_mine = norm * (3.0 * unit - 2.0 * f_mine)
        sym = 2.0 * (-0.5 * bar + scale_bar * system_mine) / norm
        pull_bar = second[1:2]
        sym = sym - (scale / total) * pull_bar
        pull_mine = self.vcol[mine, 1:2] - jnp.sum(pull_bar, axis=1, keepdims=True) / total
        mix = t_ref[mine, :] + self.vcol[mine, 0:1] / scale
        row_weights = first[3:4] + jnp.sum(second[0:1], axis=1, keepdims=True) / scale
        mix = mix + (1.0 - row_weights) / total
        observed = (self.prec[...] / scale) * (
            mm3(split(sym), split(self.anom[...])) + pull_mine * self.innov[0:1, :]
        )
        tanh = self.tanh[...]
        picked = observed * (1.0 + 0.5 * (1.0 - tanh * tanh))
        return split(mix), split(picked)


    def pull_back(self, src, first, dst, count, to_sea):
        z = self.z
        for i in range(count):
            e = first + i
            c = [self.aux[e, k : k + 1, :] for k in range(4)]
            lane = lax.broadcasted_iota(jnp.int32, (1, z.cols), 1)
            keep = 1.0 - c[0] - c[1] - c[2] - c[3]
            from_south, from_north = self.aux[e + 1, 0:1, :], self.aux[e - 1, 1:2, :]
            sea = self.aux[e, 4:5, :]
            east = pltpu.roll(jnp.broadcast_to(jnp.where(lane == 0, 0.0, c[2]), (8, z.cols)), z.cols - 1, 1)[:1]
            west = pltpu.roll(jnp.broadcast_to(jnp.where(lane == z.cols - 1, 0.0, c[3]), (8, z.cols)), 1, 1)[:1]
            if to_sea:
                keep, from_south, from_north = sea * keep, sea * from_south, sea * from_north
                east, west = sea * east, sea * west
            for part in self.chunks():
                v = src[i + 1, part, :]
                dst[i, part, :] = (
                    keep * v
                    + from_south * src[i + 2, part, :]
                    + from_north * src[i, part, :]
                    + east * pltpu.roll(v, z.cols - 1, 1)
                    + west * pltpu.roll(v, 1, 1)
                )

    def coefficient_terms(self, weight, w0, field, f0):
        z = self.z
        lane = lax.broadcasted_iota(jnp.int32, (1, z.cols), 1)
        rows = []
        for r in range(z.rows):
            sums = [0.0] * 5
            for part in self.chunks():
                w = weight[w0 + r, part, :]
                c = field[f0 + r, part, :]
                terms = [
                    w * field[f0 + r - 1, part, :],
                    w * field[f0 + r + 1, part, :],
                    w * pltpu.roll(c, 1, 1),
                    w * pltpu.roll(c, z.cols - 1, 1),
                    w * c,
                ]
                sums = [x + y for x, y in zip(sums, terms)]
            north, south, west, east, own = [jnp.sum(x, axis=0, keepdims=True) for x in sums]
            west = jnp.where(lane == 0, 0.0, west)
            east = jnp.where(lane == z.cols - 1, 0.0, east)
            rows.append([north - own, south - own, west - own, east - own])
        return rows


def kernel(z, *refs):
    names = ["prior", "cot", "stencil", "sea", "sites", "data", "prec", "grad", "coef"]
    names += list(scratch_of(z)) + ["corr"]
    g = Step(z, dict(zip(names, refs)))
    scale = jnp.sqrt(jnp.float32(z.total - 1))
    s, m = g.s_id, g.m_id
    r, ext = z.rows, z.rows + 4
    mine = pl.ds(pl.multiple_of(m * z.members, z.members), z.members)

    loads = []
    for i in range(r):
        loads.append(pltpu.make_async_copy(g.prior.at[i], g.pext.at[2 + i], g.own.at[0, i]))
    for i in range(r):
        loads.append(pltpu.make_async_copy(g.cot.at[i], g.cotf.at[i, mine], g.own.at[1, i]))
    for copy in loads:
        copy.start()
    for e in (0, 1, ext - 2, ext - 1):
        g.pext[e] = jnp.zeros((z.members, z.cols), F32)
        g.sbext[e] = jnp.zeros((z.members, z.cols), F32)
        g.aux[e] = jnp.zeros((8, z.cols), F32)
    for i in range(r):
        g.aux[2 + i, 0:4, :] = g.stencil[:, i, :]
        g.aux[2 + i, 4:5, :] = g.sea[i : i + 1, :].astype(F32)
        g.aux[2 + i, 5:8, :] = jnp.zeros((3, z.cols), F32)
    entered = g.barrier()
    for copy in loads[:r]:
        copy.wait()
    entered()
    halo = g.halo_send(g.pext, g.halo)
    aux_halo = g.halo_send(g.aux, g.aux_halo)
    for copy in loads[r:]:
        copy.wait()
    cot_forward, cot_wait = g.pair_gather(lambda which: g.cotf.at[:, pl.ds(pl.multiple_of(which * z.members, z.members), z.members)], g.cot_sem)
    g.mark_sites()
    aux_halo()
    cot_forward()
    halo()

    g.advance(g.pext, 1, g.fext, r + 2)
    g.advance(g.fext, 2, g.state, r)
    g.obsf[mine, :] = g.observe()
    obs_forward, obs_wait = g.pair_gather(lambda which: g.obsf.at[pl.ds(pl.multiple_of(which * z.members, z.members), z.members)], g.obs_sem)
    own = [jnp.sum(g.state[i], axis=0, keepdims=True) for i in range(r)]
    own += [jnp.zeros((-r % 8, z.cols), F32)] * (r % 8 > 0)
    g.sums[m] = jnp.concatenate(own, axis=0)
    sums_wait = g.mem_send(g.sums, g.sum_sem)

    cot_wait()
    for i in range(r):
        g.chi[i], g.clo[i] = split(g.cotf[i])
    dev = [split((g.state[i] - own[i] / z.members) / scale) for i in range(r)]
    d_copies = []
    order = [k for k in range(1, z.n_mem) if 2 * k <= z.n_mem] + [0] + [k for k in range(1, z.n_mem) if 2 * k > z.n_mem]
    for k in order:
        there = lax.rem(m + k, z.n_mem)
        rows = pl.ds(pl.multiple_of(there * z.members, z.members), z.members)
        part = mm3_t(dev[0], (g.chi[0, rows, :], g.clo[0, rows, :]))
        for i in range(1, r):
            part = part + mm3_t(dev[i], (g.chi[i, rows, :], g.clo[i, rows, :]))
        g.dmat[k] = part
        if 0 < 2 * k <= z.n_mem:
            back = z.n_mem - k
            copy = remote(g.dmat.at[k], g.dx.at[back], g.d_sem.at[0, k], g.d_sem.at[1, k], s, there)
            copy.start()
            d_copies.append(copy)
    obs_forward()
    sums_wait()
    obs_wait()
    for copy in d_copies:
        copy.wait_recv()
    g.waits += [(copy, None) for copy in d_copies]
    g.pack(scale)
    small = g.reduce_scatter()
    g.all_gather(small)

    mix, picked = g.analyse(scale)
    for i in range(r):
        mark = g.hot[i]
        spread = plain_t(picked[0], mark) + plain_t(picked[1], mark)
        g.sbext[2 + i] = g.aux[2 + i, 4:5, :] * (mm3(mix, (g.chi[i], g.clo[i])) + spread)
    bar_halo = g.halo_send(g.sbext, g.bar_halo)
    second = g.coefficient_terms(g.sbext, 2, g.fext, 1)
    bar_halo()
    g.pull_back(g.sbext, 1, g.fbar, r + 2, True)
    firsts = g.coefficient_terms(g.fbar, 1, g.pext, 2)
    g.cbuf[m] = jnp.concatenate(
        [second[i][k] + firsts[i][k] for k in range(4) for i in range(r)], axis=0
    )
    c_wait = g.mem_send(g.cbuf, g.c_sem)
    g.pull_back(g.fbar, 2, g.grad, r, False)
    c_wait()
    both = g.cbuf[0]
    for k in range(1, z.n_mem):
        both = both + g.cbuf[k]
    both = both / jnp.sqrt(jnp.float32(z.total))
    for k in range(4):
        g.coef[k] = both[k * r : (k + 1) * r]
    g.finish_sends()


def local(n_space, n_mem, prior, stencil, sea_mask, sites, data, precision, cotangent):
    z = Sizes(n_space, n_mem, prior, sites)
    any_spec = pl.BlockSpec(memory_space=pl.ANY)
    grad, coef = pl.pallas_call(
        functools.partial(kernel, z),
        out_shape=(
            jax.ShapeDtypeStruct((z.rows, z.members, z.cols), F32),
            jax.ShapeDtypeStruct((4, z.rows, z.cols), F32),
        ),
        in_specs=[any_spec, any_spec] + [VMEM_SPEC] * 5,
        out_specs=(VMEM_SPEC, VMEM_SPEC),
        scratch_shapes=list(scratch_of(z).values()) + [pltpu.VMEM((8 * pl.cdiv(n_mem, 8), z.total), F32)],
        compiler_params=pltpu.CompilerParams(
            collective_id=1, has_side_effects=True, vmem_limit_bytes=60 * 1024 * 1024
        ),
        name="adjoint",
    )(
        jnp.transpose(prior, (1, 0, 2)), jnp.transpose(cotangent, (1, 0, 2)),
        stencil, sea_mask, sites, data[None], precision[None],
    )
    return jnp.transpose(grad, (1, 0, 2)), coef


def solution(mesh):
    placed = (
        P("mem", "space", None),
        P(None, "space", None),
        P("space", None),
        P("space", None),
        P("space"),
        P("space"),
        P("mem", "space", None),
    )
    return jax.shard_map(
        functools.partial(local, mesh.shape["space"], mesh.shape["mem"]),
        mesh=mesh,
        in_specs=placed,
        out_specs=(P("mem", "space", None), P(None, "space", None)),
        check_vma=False,
    )
```

profile of v0, /device:TPU:5, one launch (start us, length us, event | category | flops | bytes accessed | tf_op | source)
XLA Modules:
  0.0 66.9 jit_solution(9081215637435987642)
XLA Ops:
  0.6 1.8 %copy_bitcast_fusion = (f32[4,128,128]{2,1,0:T(8,128)}, f32[4,128,128]{2,1,0:T(8,128)}) fusion(f32[128,4,128]{2,1,0:T(4,128)} %param.13, f32[128,4,128]{2,1,0:T(4,128)} %param.7), kind=kLoop, calls=%fused_computation | loop fusion | bytes 1048576 | tf_op jit(solution)/shard_map/transpose | solution.py:725
  2.5 62.0 %adjoint.1 = (f32[4,128,128]{2,1,0:T(8,128)}, f32[4,4,128]{2,1,0:T(4,128)}) custom-call(f32[4,128,128]{2,1,0:T(8,128)} %get-tuple-element.9.refs_0_, f32[4,128,128]{2,1,0:T(8,128)} %get-tuple-element.8.refs_1_, f32[4,4,128]{2,1,0:T(4,128)} %refs_2_.1, s32[4,128]{1,0:T(4,128)} %refs_3_.1, s32[1,128]{1,0:T(1,128)} %refs_4_.1, f32[1,128]{1,0:T(1,128)} %bitcast.8, ...), custom_call_target="tpu_custom_call" | custom-call | tf_op jit(solution)/shard_map/adjoint/pallas_call | solution.py:711
  64.5 0.0 copy-start
  64.5 1.8 %copy.11 = f32[128,4,128]{2,1,0:T(4,128)} copy(f32[128,4,128]{2,0,1:T(8,128)} %bitcast.7) | data formatting | bytes 524288
  66.3 0.0 copy-done
  66.3 0.6 copy.15
Async XLA Ops:
  64.5 1.8 %copy-start = (f32[4,4,128]{2,1,0:T(4,128)S(1)}, f32[4,4,128]{2,1,0:T(4,128)}, u32[]{:S(2)}) copy-start(f32[4,4,128]{2,1,0:T(4,128)} %get-tuple-element.13) | copy-start | bytes 24580
where the time goes:
time: 67.3 us; the launch traced here: 66.9 us
  Pallas kernels  62 us (92%)
  local copies, waits for them, and re-layouts  4.27 us (6%)
    pallas_call x1, Pallas kernels, local(): pl.pallas_call(functools.partial(kernel, z), out_shape=(jax.ShapeDtypeStr...  62 us
    unnamed x4, local copies, waits for them, and re-layouts  2.43 us
    transpose x1, local copies, waits for them, and re-layouts, local(): jnp.transpose(cotangent, (1, 0, 2))  1.84 us

commit v1 on v0

v1 whole, which is shorter than its diff:
```python
import functools
import jax
import jax.numpy as jnp
from jax import lax
from jax.experimental import pallas as pl
from jax.experimental.pallas import tpu as pltpu
from jax.sharding import PartitionSpec as P

MESH = pl.DeviceIdType.MESH
F32 = jnp.float32
GRANT = 48 * 1024 * 1024
BF16 = jnp.bfloat16
VMEM_SPEC = pl.BlockSpec(memory_space=pltpu.VMEM)


def remote(src, dst, send, recv, s, m):
    return pltpu.make_async_remote_copy(
        src_ref=src, dst_ref=dst, send_sem=send, recv_sem=recv, device_id=(s, m), device_id_type=MESH
    )


def split(x):
    lead = x.astype(BF16)
    return lead, (x - lead.astype(F32)).astype(BF16)


def split3(x):
    lead = x.astype(BF16)
    rest = x - lead.astype(F32)
    middle = rest.astype(BF16)
    return lead, middle, (rest - middle.astype(F32)).astype(BF16)


def plain(a, b):
    return jnp.dot(a, b, preferred_element_type=F32)


def plain_t(a, b):
    return lax.dot_general(a, b, (((1,), (1,)), ((), ())), preferred_element_type=F32)


def mm3(a, b):
    return plain(a[0], b[0]) + (plain(a[0], b[1]) + plain(a[1], b[0]))


def mm3_t(a, b):
    return plain_t(a[0], b[0]) + (plain_t(a[0], b[1]) + plain_t(a[1], b[0]))


def whole_sum(x):
    return jnp.sum(jnp.sum(x, axis=0, keepdims=True), axis=1, keepdims=True)


def eye(size):
    return lax.broadcasted_iota(jnp.int32, (size, size), 0) == lax.broadcasted_iota(
        jnp.int32, (size, size), 1
    )


class Sizes:
    def __init__(self, n_space, n_mem, prior, sites):
        self.n_space, self.n_mem = n_space, n_mem
        self.members, self.rows, self.cols = prior.shape
        self.total = self.members * n_mem
        self.sites = sites.shape[-1]
        self.near = 2 if n_space % 2 == 0 else 1
        self.far = n_space // self.near
        self.half = 2 if n_mem % 2 == 0 else 1
        self.wide = n_mem // self.half
        self.group = max(1, self.far // 4)
        self.groups = self.far // self.group
        self.height = n_mem // 2 * self.members // n_space
        self.lines = 8 * pl.cdiv(4 + n_mem, 8)


def scratch_of(z):
    dma = pltpu.SemaphoreType.DMA
    ext = z.rows + 4
    v = lambda *shape: pltpu.VMEM(shape, F32)
    b = lambda *shape: pltpu.VMEM(shape, BF16)
    square = (z.total, z.total)
    half_square = (z.n_space, z.height, z.members)
    gathered = (z.n_mem, z.far, z.near, z.height, z.members)
    found = dict(
        stencil=v(4, z.rows, z.cols),
        sea=pltpu.VMEM((z.rows, z.cols), jnp.int32),
        sites=pltpu.VMEM((1, z.sites), jnp.int32),
        data=v(1, z.sites),
        prec=v(1, z.sites),
        few=dma((5,)),
        pext=v(ext, z.members, z.cols),
        aux=v(ext, 8, z.cols),
        cotf=v(z.rows, z.total, z.cols),
        chi=b(z.rows, z.total, z.cols),
        clo=b(z.rows, z.total, z.cols),
        fext=v(z.rows + 2, z.members, z.cols),
        state=v(z.rows, z.members, z.cols),
        hot=b(ext, z.cols, z.sites),
        obsf=v(z.n_mem, z.members, z.sites),
        tanh=v(z.members, z.sites),
        ahi=b(z.total, z.sites),
        alo=b(z.total, z.sites),
        innov=v(8, z.sites),
        sums=v(z.n_mem, 8 * pl.cdiv(z.rows, 8), z.cols),
        dmat=v(z.n_mem, z.members, z.members),
        dx=v(z.n_mem, z.members, z.members),
        vec=v(z.lines, z.members),
        vbuf=v(z.n_space, z.lines, z.members),
        vout=v(z.n_mem, z.lines, z.members),
        f=v(*square),
        g=v(*square),
        fg=v(*square),
        s=v(*square),
        weigh=v(*square),
        fh=b(*square), fl=b(*square),
        f2h=b(*square), f2l=b(*square),
        gh=b(*square), gl=b(*square),
        sh=b(*square), sl=b(*square),
        lh=b(3 * z.members, z.total), ll=b(3 * z.members, z.total),
        vcol=v(z.total, z.lines),
        sbext=v(ext, z.members, z.cols),
        mixed=v(ext, z.members, z.cols),
        picked=v(3, z.members, z.sites),
        fbar=v(z.rows + 2, z.members, z.cols),
        cbuf=v(z.n_mem, 4 * z.rows, z.cols),
        own=dma((2, z.rows)),
        halo=dma((2, 2)),
        aux_halo=dma((2, 2)),
        bar_halo=dma((2, 2)),
        pick_sem=dma((2, 2)),
        cot_sem=dma((2, z.half, z.wide)),
        obs_sem=dma((2, z.n_mem)),
        sum_sem=dma((2, z.n_mem)),
        d_sem=dma((2, z.n_mem)),
        v_sem=dma((2, z.n_space)),
        vg_sem=dma((2, z.n_mem)),
        c_sem=dma((2, z.n_mem)),
    )
    for tag in ("gram", "cross"):
        found[tag + "_src"] = v(*half_square)
        found[tag + "_buf"] = v(*half_square)
        found[tag + "_out"] = v(*gathered)
        found[tag + "_rs"] = dma((2, z.n_space))
        found[tag + "_a"] = dma((2, z.far))
        found[tag + "_x"] = dma((2, z.near, z.wide, z.groups))
        found[tag + "_q"] = dma((2, z.half, z.near, z.wide, z.groups))
    return found


class Reduction:
    def __init__(self, g, tag):
        self.g, self.z = g, g.z
        for name in ("src", "buf", "out", "rs", "a", "x", "q"):
            setattr(self, name, getattr(g, tag + "_" + name))
        z = g.z
        self.a_id, self.b_id = g.s_id // z.near, lax.rem(g.s_id, z.near)
        self.p_id, self.q_id = g.m_id // z.half, lax.rem(g.m_id, z.half)

    def scatter(self):
        z, s, m = self.z, self.g.s_id, self.g.m_id
        self.copies = []
        for k in range(1, z.n_space):
            to = lax.rem(s + k, z.n_space)
            self.copies.append(
                remote(self.src.at[to], self.buf.at[s], self.rs.at[0, k], self.rs.at[1, k], to, m)
            )
            self.copies[-1].start()
        self.g.waits += [(copy, None) for copy in self.copies]

    def start(self):
        z, s, m = self.z, self.g.s_id, self.g.m_id
        a, b = self.a_id, self.b_id
        self.buf[s] = self.src[s]
        for copy in self.copies:
            copy.wait_recv()
        total = self.buf[0]
        for k in range(1, z.n_space):
            total = total + self.buf[k]
        self.out[m, a, b] = total
        piece = self.out.at[m, a, b]
        stage = []
        for k in range(1, z.far):
            to = lax.rem(a + k, z.far) * z.near + b
            stage.append(remote(piece, piece, self.a.at[0, k], self.a.at[1, k], to, m))
            stage[-1].start()
        self.g.waits += [(copy, None) for copy in stage]
        if z.group == 1:
            self.steps = [([], a)] + [
                ([stage[k - 1]], lax.rem(a + z.far - k, z.far)) for k in range(1, z.far)
            ]
            self.forward(0)
        else:
            self.steps = [(stage if n == 0 else [], n * z.group) for n in range(z.groups)]

    def forward(self, index):
        z, s, m = self.z, self.g.s_id, self.g.m_id
        needs, start = self.steps[index]
        for copy in needs:
            copy.wait_recv()
        piece = self.out.at[m, pl.ds(start, z.group), self.b_id]
        for kb, kp in self.offsets():
            to_s = self.a_id * z.near + lax.rem(self.b_id + kb, z.near)
            to_m = lax.rem(self.p_id + kp, z.wide) * z.half + self.q_id
            self.send(piece, self.x.at[0, kb, kp, index], self.x.at[1, kb, kp, index], to_s, to_m)
        self.beside(piece, 0, 0, index)

    def forward_all(self):
        for index in range(1 if self.z.group == 1 else 0, self.z.groups):
            self.forward(index)

    def offsets(self):
        z = self.z
        return [(kb, kp) for kb in range(z.near) for kp in range(z.wide) if kb or kp]

    def send(self, piece, *where):
        copy = remote(piece, piece, *where)
        copy.start()
        self.g.waits.append((copy, None))

    def beside(self, piece, kb, kp, index):
        z = self.z
        for kq in range(1, z.half):
            to = self.p_id * z.half + lax.rem(self.q_id + kq, z.half)
            self.send(
                piece, self.q.at[0, kq, kb, kp, index], self.q.at[1, kq, kb, kp, index], self.g.s_id, to
            )

    def piece_of(self, kb, kp, kq, index):
        z = self.z
        which_b = lax.rem(self.b_id + z.near - kb, z.near)
        which_p = lax.rem(self.p_id + z.wide - kp, z.wide)
        which_q = lax.rem(self.q_id + z.half - kq, z.half)
        return self.out.at[which_p * z.half + which_q, pl.ds(self.steps[index][1], z.group), which_b]

    def pass_on(self):
        for index in range(self.z.groups):
            for kb, kp in self.offsets():
                piece = self.piece_of(kb, kp, 0, index)
                self.arrived(piece, self.x.at[0, kb, kp, index], self.x.at[1, kb, kp, index])
                self.beside(piece, kb, kp, index)

    def arrived(self, piece, send, recv):
        remote(piece, piece, send, recv, self.g.s_id, self.g.m_id).wait_recv()

    def finish(self):
        z = self.z
        for index in range(z.groups):
            for kb in range(z.near):
                for kp in range(z.wide):
                    for kq in range(1, z.half):
                        self.arrived(
                            self.piece_of(kb, kp, kq, index),
                            self.q.at[0, kq, kb, kp, index], self.q.at[1, kq, kb, kp, index],
                        )

    def whole(self, i):
        z = self.z
        return self.out[i].reshape(z.n_mem // 2 * z.members, z.members)


class Step:
    def __init__(self, z, refs):
        self.z = z
        self.__dict__.update(refs)
        self.s_id, self.m_id = lax.axis_index("space"), lax.axis_index("mem")
        self.lo = lax.rem(self.m_id, z.n_mem // 2)
        self.hi = self.m_id // (z.n_mem // 2)
        self.waits = []

    def finish_sends(self):
        for copy, when in self.waits:
            if when is None:
                copy.wait_send()
            else:
                pl.when(when)(copy.wait_send)

    def barrier(self):
        z, s, m = self.z, self.s_id, self.m_id
        peers = [(lax.rem(s + k, z.n_space), m) for k in range(1, z.n_space)]
        peers += [(s, lax.rem(m + k, z.n_mem)) for k in range(1, z.n_mem)]
        a, b = s // z.near, lax.rem(s, z.near)
        p, q = m // z.half, lax.rem(m, z.half)
        for kb in range(1, z.near):
            for kp in range(1, z.wide):
                peers.append((
                    a * z.near + lax.rem(b + kb, z.near), lax.rem(p + kp, z.wide) * z.half + q
                ))
        barrier = pltpu.get_barrier_semaphore()
        for peer in peers:
            pl.semaphore_signal(barrier, inc=1, device_id=peer, device_id_type=MESH)
        return lambda: pl.semaphore_wait(barrier, len(peers))

    def between(self, up_src, up_dst, down_src, down_dst, sem):
        z, s, m = self.z, self.s_id, self.m_id
        has_low, has_high = s > 0, s < z.n_space - 1
        up = remote(up_src, up_dst, sem.at[0, 0], sem.at[1, 0], s + 1, m)
        down = remote(down_src, down_dst, sem.at[0, 1], sem.at[1, 1], s - 1, m)
        pl.when(has_high)(up.start)
        pl.when(has_low)(down.start)
        self.waits += [(up, has_high), (down, has_low)]

        def wait():
            pl.when(has_low)(up.wait_recv)
            pl.when(has_high)(down.wait_recv)

        return wait

    def halo_send(self, ref, sem):
        r = self.z.rows
        at = lambda row: ref.at[pl.ds(row, 2)]
        return self.between(at(r), at(0), at(2), at(r + 2), sem)

    def pair_gather(self, part, sem):
        z, s, m = self.z, self.s_id, self.m_id
        p, q = m // z.half, lax.rem(m, z.half)
        across = [lax.rem(p + k, z.wide) * z.half + q for k in range(1, z.wide)]
        beside = [p * z.half + lax.rem(q + k, z.half) for k in range(1, z.half)]
        mine = part(m)
        hops, sides = [], []
        for k, to in enumerate(across):
            hops.append(remote(mine, mine, sem.at[0, 0, k + 1], sem.at[1, 0, k + 1], s, to))
            hops[-1].start()
        for k, to in enumerate(beside):
            sides.append(remote(mine, mine, sem.at[0, k + 1, 0], sem.at[1, k + 1, 0], s, to))
            sides[-1].start()

        def forward():
            for kp, hop in enumerate(hops):
                hop.wait_recv()
                piece = part(lax.rem(p + z.wide - kp - 1, z.wide) * z.half + q)
                for k, to in enumerate(beside):
                    copy = remote(
                        piece, piece, sem.at[0, k + 1, kp + 1], sem.at[1, k + 1, kp + 1], s, to
                    )
                    copy.start()
                    sides.append(copy)

        def wait():
            for copy in sides:
                copy.wait_recv()
            self.waits.extend((copy, None) for copy in hops + sides)

        return forward, wait

    def mem_send(self, ref, sem):
        z, s, m = self.z, self.s_id, self.m_id
        copies = []
        for k in range(1, z.n_mem):
            to = lax.rem(m + k, z.n_mem)
            copies.append(remote(ref.at[m], ref.at[m], sem.at[0, k], sem.at[1, k], s, to))
            copies[-1].start()

        def wait():
            for copy in copies:
                copy.wait_recv()
            self.waits.extend((copy, None) for copy in copies)

        return wait

    def block(self, which):
        size = self.z.members
        return pl.ds(pl.multiple_of(which * size, size), size)


    def coefficients(self, e):
        z = self.z
        c = [self.aux[e, k : k + 1, :] for k in range(4)]
        sea = self.aux[e, 4:5, :]
        lane = lax.broadcasted_iota(jnp.int32, (1, z.cols), 1)
        keep = sea * (1.0 - c[0] - c[1] - c[2] - c[3])
        west = jnp.where(lane == 0, 0.0, c[2])
        east = jnp.where(lane == z.cols - 1, 0.0, c[3])
        return keep, sea * c[0], sea * c[1], sea * west, sea * east

    def chunks(self):
        size = min(32, self.z.members)
        return [pl.ds(k, size) for k in range(0, self.z.members, size)]

    def advance(self, src, first, dst, count):
        z = self.z
        for i in range(count):
            keep, north, south, west, east = self.coefficients(first + i)
            for part in self.chunks():
                v = src[i + 1, part, :]
                dst[i, part, :] = (
                    keep * v
                    + north * src[i, part, :]
                    + south * src[i + 2, part, :]
                    + west * pltpu.roll(v, 1, 1)
                    + east * pltpu.roll(v, z.cols - 1, 1)
                )

    def observe(self):
        z = self.z
        picked = jnp.zeros((z.members, z.sites), F32)
        for r in range(z.rows):
            for piece in split3(self.state[r]):
                picked = picked + plain(piece, self.hot[2 + r])
        tanh = jnp.tanh(picked)
        self.tanh[...] = tanh
        return picked + 0.5 * tanh

    def mark(self, e, row, sites):
        z = self.z
        cell = lax.broadcasted_iota(jnp.int32, (z.cols, z.sites), 0) + row * z.cols
        self.hot[e] = jnp.where(cell == sites, 1.0, 0.0).astype(BF16)

    def mark_sites(self):
        for r in range(self.z.rows):
            self.mark(2 + r, r, self.sites[...])

    def mark_sites_beside(self):
        r = self.z.rows
        low, high = (self.aux[e, 5:6, :].astype(jnp.int32) for e in (1, r + 2))
        for k in range(2):
            self.mark(k, r - 2 + k, low)
            self.mark(r + 2 + k, k, high)

    def spread(self, slot, rows):
        hi, lo = split(self.picked[slot])
        for e in rows:
            field = self.mixed[e] + plain_t(hi, self.hot[e]) + plain_t(lo, self.hot[e])
            self.sbext[e] = self.aux[e, 4:5, :] * field


    def fold(self, block):
        size = self.z.members
        half = size // 2
        bottom = pltpu.roll(block[half:], half, 1)
        lane = lax.broadcasted_iota(jnp.int32, (half, size), 1)
        line = lax.broadcasted_iota(jnp.int32, (half, size), 0)
        return jnp.where(lane < line, bottom, block[:half])

    def unfold(self, folded, diagonal):
        size = self.z.members
        half = size // 2
        wide = jnp.concatenate([folded, pltpu.roll(folded, half, 1)], axis=0)
        lane = lax.broadcasted_iota(jnp.int32, (size, size), 1)
        line = lax.broadcasted_iota(jnp.int32, (size, size), 0)
        above, below = lane - line, lane - half
        straight = ((line < half) & (above >= 0)) | ((line >= half) & (below >= 0) & (above < 0))
        block = jnp.where(straight, wide, wide.T)
        return jnp.where((line >= half) & (above == 0), diagonal, block)

    def cross_rows(self, dev):
        z, s, m = self.z, self.s_id, self.m_id
        n, size = z.n_mem, z.members
        half = size // 2
        self.d_copies = []
        mean_bar = jnp.zeros((size, 1), F32)
        for k in list(range(n - 1, 0, -1)) + [0]:
            there = lax.rem(m + k, n)
            rows = self.block(there)
            part = mm3_t(dev[0], (self.chi[0, rows, :], self.clo[0, rows, :]))
            for i in range(1, z.rows):
                part = part + mm3_t(dev[i], (self.chi[i, rows, :], self.clo[i, rows, :]))
            mean_bar = mean_bar + jnp.sum(part, axis=1, keepdims=True)
            if 2 * k == n:
                part = jnp.where(self.hi == 0, part, part.T)
            self.dmat[k] = part
            copy = None
            if 2 * k > n:
                copy = remote(
                    self.dmat.at[k], self.dx.at[n - k], self.d_sem.at[0, k], self.d_sem.at[1, k], s, there
                )
            elif 2 * k == n:
                theirs = pl.ds(pl.multiple_of((1 - self.hi) * half, half), half)
                copy = remote(
                    self.dmat.at[k, theirs], self.dx.at[k, pl.ds(0, half)],
                    self.d_sem.at[0, k], self.d_sem.at[1, k], s, there,
                )
            if copy is not None:
                copy.start()
                self.d_copies.append(copy)
        self.waits += [(copy, None) for copy in self.d_copies]
        return mean_bar

    def pack_gram(self, scale, mean_bar, own_sums):
        z, m = self.z, self.m_id
        n, size = z.n_mem, z.members
        half = size // 2
        mean = jnp.zeros((1, z.sites), F32)
        for k in range(n):
            mean = mean + jnp.sum(self.obsf[k], axis=0, keepdims=True)
        mean = mean / z.total
        prec = self.prec[...]
        innov = prec * (self.data[...] - mean)
        self.innov[0:1, :] = innov
        for k in range(n):
            rows = slice(k * size, (k + 1) * size)
            self.ahi[rows, :], self.alo[rows, :] = split((self.obsf[k] - mean) * (prec / scale))
        anom = lambda rows: (self.ahi[rows, :], self.alo[rows, :])
        mine = anom(self.block(m))
        diag = mm3_t(mine, mine)
        parts = [self.fold(diag)]
        base = self.lo * size + self.hi * half
        upper = anom(pl.ds(pl.multiple_of(base, half), half))
        parts.append(mm3_t(upper, anom(self.block(self.lo + n // 2))))
        for k in range(1, n // 2):
            parts.append(mm3_t(mine, anom(self.block(lax.rem(m + k, n)))))
        self.gram_src[...] = jnp.concatenate(parts, axis=0).reshape(z.n_space, z.height, size)

        cross = self.dmat[0]
        self.cross_diag = 0.5 * (cross + cross.T)
        exact = (self.obsf[m] - mean) * (prec / scale)
        lane = lax.broadcasted_iota(jnp.int32, (size, size), 1)
        diagonal = lambda x: jnp.sum(jnp.where(eye(size), x, 0.0), axis=1, keepdims=True)
        pull = jnp.sum(exact * innov, axis=1, keepdims=True)
        columns = [pull, mean_bar, diagonal(self.cross_diag), diagonal(diag)]
        stacked = jnp.zeros((size, size), F32)
        for k, column in enumerate(columns):
            stacked = jnp.where(lane == k, column, stacked)
        total = self.sums[0]
        for k in range(1, n):
            total = total + self.sums[k]
        term = None
        for r in range(z.rows):
            lacks = (own_sums[r] / size - total[r : r + 1] / z.total) / scale
            this = mm3_t(split(jnp.broadcast_to(lacks, (8, z.cols))), (self.chi[r], self.clo[r]))
            term = this if term is None else term + this
        lines = [stacked.T[:4]] + [term[:1, k * size : (k + 1) * size] for k in range(n)]
        if z.lines > 4 + n:
            lines.append(jnp.zeros((z.lines - 4 - n, size), F32))
        self.vec[...] = jnp.concatenate(lines, axis=0)

    def pack_cross(self):
        z = self.z
        n, size = z.n_mem, z.members
        half = size // 2
        for copy in self.d_copies:
            copy.wait_recv()
        parts = [self.fold(self.cross_diag)]
        ours = pl.ds(pl.multiple_of(self.hi * half, half), half)
        parts.append(0.5 * (self.dmat[n // 2, ours] + self.dx[n // 2, pl.ds(0, half)]))
        for k in range(1, n // 2):
            parts.append(0.5 * (self.dmat[k] + self.dx[k].T))
        self.cross_src[...] = jnp.concatenate(parts, axis=0).reshape(z.n_space, z.height, size)

    def send_lines(self):
        z, s, m = self.z, self.s_id, self.m_id
        self.tiny = []
        for k in range(1, z.n_space):
            to = lax.rem(s + k, z.n_space)
            self.tiny.append(
                remote(self.vec, self.vbuf.at[s], self.v_sem.at[0, k], self.v_sem.at[1, k], to, m)
            )
            self.tiny[-1].start()
        self.waits += [(copy, None) for copy in self.tiny]

    def sum_lines(self):
        self.vbuf[self.s_id] = self.vec[...]
        for copy in self.tiny:
            copy.wait_recv()
        vec = self.vbuf[0]
        for k in range(1, self.z.n_space):
            vec = vec + self.vbuf[k]
        self.vout[self.m_id] = vec
        return self.mem_send(self.vout, self.vg_sem)

    def blocks_of(self, reduction, line):
        z = self.z
        n, size = z.n_mem, z.members
        half = size // 2
        wholes = [reduction.whole(i) for i in range(n)]
        for i in range(n):
            yield i, i, self.unfold(wholes[i][:half], self.vout[i, line : line + 1, :])
        for i in range(n // 2):
            j = i + n // 2
            yield i, j, jnp.concatenate([wholes[i][half:size], wholes[j][half:size]], axis=0)
        for i in range(n):
            for k in range(1, n // 2):
                yield i, (i + k) % n, wholes[i][k * size : (k + 1) * size]


    def transform(self, scale, gram):
        z, m = self.z, self.m_id
        n, size, total = z.n_mem, z.members, z.total
        mine = self.block(m)
        col = lambda k: slice(k * size, (k + 1) * size)
        squares = jnp.zeros((size, size), F32)
        for i, j, block in self.blocks_of(gram, 3):
            if i == j:
                block = block + eye(size).astype(F32)
                squares = squares + block * block
            else:
                self.f[col(j), col(i)] = block.T
                squares = squares + 2.0 * (block * block)
            self.f[col(i), col(j)] = block
        norm = jnp.sqrt(whole_sum(squares))
        root = jnp.sqrt(norm)
        identity = eye(total).astype(F32)
        f = 1.5 * identity - (0.5 / norm) * self.f[...]
        self.f[...] = f
        self.fh[...], self.fl[...] = split(f)
        f_split = (self.fh[...], self.fl[...])
        f2 = mm3(f_split, f_split)
        self.f2h[...], self.f2l[...] = split(f2)
        g = f2 - 1.5 * self.f[...]
        self.g[...] = g
        self.gh[...], self.gl[...] = split(g)
        g_split = (self.gh[...], self.gl[...])
        yield
        p = 1.5 * self.f[...] + mm3((self.f2h[...], self.f2l[...]), g_split)
        self.s[...] = p
        p_split = split(p)
        kind = lax.broadcasted_iota(jnp.int32, (z.lines, size), 0)
        self.lines = []
        for i in range(n):
            lines = self.vout[i]
            lacks = jnp.sum(jnp.sum(lines[4 : 4 + n], axis=0, keepdims=True), axis=1, keepdims=True)
            self.lines.append(jnp.where(kind == 1, lines + lacks, jnp.where(kind == 3, 1.0, lines)))
        rows = jnp.concatenate(self.lines, axis=1)
        self.first = mm3(split(rows), p_split) / root
        second = mm3(split(self.first), p_split) / root
        self.vcol[...] = second.T
        self.pull_bar = second[1:2]
        self.pull_mine = self.vcol[mine, 1:2] - jnp.sum(self.pull_bar, axis=1, keepdims=True) / total
        mix = self.s[mine, :] / root + self.vcol[mine, 0:1] / scale
        row_weights = self.first[3:4] + jnp.sum(second[0:1], axis=1, keepdims=True) / scale
        mix = split(mix + (1.0 - row_weights) / total)
        for r in range(z.rows):
            self.mixed[2 + r] = mm3(mix, (self.chi[r], self.clo[r]))
        bar_halo = self.halo_send(self.mixed, self.bar_halo)
        self.fg[...] = mm3((self.fh[...], self.fl[...]), g_split)
        self.weigh[...] = 2.25 * identity + 4.5 * (self.fg[...] + self.f[...] - self.s[...])
        self.norm, self.root = norm, root
        for k, ref in enumerate((self.f, self.g, self.fg)):
            rows = slice(k * size, (k + 1) * size)
            self.lh[rows, :], self.ll[rows, :] = split(self.centred(ref))
        yield bar_halo

    def centred(self, ref):
        return ref[self.block(self.m_id), :] - jnp.sum(ref[...], axis=0, keepdims=True) / self.z.total

    def respond(self, scale, cross):
        z, m = self.z, self.m_id
        n, size, total = z.n_mem, z.members, z.total
        col = lambda k: slice(k * size, (k + 1) * size)
        norm, root = self.norm, self.root
        turned = [x.T for x in self.lines]
        first_t = self.first.T
        for i, j, block in self.blocks_of(cross, 2):
            block = (scale / root) * (
                block + 0.5 * (self.lines[i][4 + j : 5 + j] + turned[j][:, 4 + i : 5 + i])
            ) + (0.5 / root) * (
                turned[i][:, 1:2] * self.first[0:1, col(j)]
                + first_t[col(i), 0:1] * self.lines[j][1:2]
                + first_t[col(i), 1:2] * self.lines[j][0:1]
                + turned[i][:, 0:1] * self.first[1:2, col(j)]
            )
            self.s[col(i), col(j)] = block
            if i != j:
                self.s[col(j), col(i)] = block.T
        scale_bar = whole_sum(self.s[...] * self.weigh[...]) / norm
        self.sh[...], self.sl[...] = split(self.s[...])
        s_split = (self.sh[...], self.sl[...])
        s_mine = self.centred(self.s)
        f_split = (self.fh[...], self.fl[...])
        through = mm3((self.lh[...], self.ll[...]), s_split)
        bar = 1.5 * s_mine + through[2 * size :]
        bar = bar + mm3(split(mm3(split(s_mine), f_split)), (self.gh[...], self.gl[...]))
        bar = bar + mm3(split(through[:size]), (self.f2h[...], self.f2l[...]))
        bar = bar + mm3(split(through[size : 2 * size]), f_split)
        unit = (
            lax.broadcasted_iota(jnp.int32, (size, total), 0) + m * size
            == lax.broadcasted_iota(jnp.int32, (size, total), 1)
        ).astype(F32) - 1.0 / total
        sym = 2.0 * scale_bar * (3.0 * unit - 2.0 * self.centred(self.f)) - bar / norm
        sym = sym - (scale / total) * self.pull_bar
        observed = (self.prec[...] / scale) * (
            mm3(split(sym), (self.ahi[...], self.alo[...])) + self.pull_mine * self.innov[0:1, :]
        )
        tanh = self.tanh[...]
        return observed * (1.0 + 0.5 * (1.0 - tanh * tanh))


    def pull_back(self, src, first, dst, rows, to_sea):
        z = self.z
        for i in rows:
            e = first + i
            c = [self.aux[e, k : k + 1, :] for k in range(4)]
            lane = lax.broadcasted_iota(jnp.int32, (1, z.cols), 1)
            keep = 1.0 - c[0] - c[1] - c[2] - c[3]
            from_south, from_north = self.aux[e + 1, 0:1, :], self.aux[e - 1, 1:2, :]
            sea = self.aux[e, 4:5, :]
            east = pltpu.roll(jnp.broadcast_to(jnp.where(lane == 0, 0.0, c[2]), (8, z.cols)), z.cols - 1, 1)[:1]
            west = pltpu.roll(jnp.broadcast_to(jnp.where(lane == z.cols - 1, 0.0, c[3]), (8, z.cols)), 1, 1)[:1]
            if to_sea:
                keep, from_south, from_north = sea * keep, sea * from_south, sea * from_north
                east, west = sea * east, sea * west
            for part in self.chunks():
                v = src[i + 1, part, :]
                dst[i, part, :] = (
                    keep * v
                    + from_south * src[i + 2, part, :]
                    + from_north * src[i, part, :]
                    + east * pltpu.roll(v, z.cols - 1, 1)
                    + west * pltpu.roll(v, 1, 1)
                )

    def coefficient_terms(self, weight, w0, field, f0):
        z = self.z
        lane = lax.broadcasted_iota(jnp.int32, (1, z.cols), 1)
        rows = []
        for r in range(z.rows):
            sums = [0.0] * 5
            for part in self.chunks():
                w = weight[w0 + r, part, :]
                c = field[f0 + r, part, :]
                terms = [
                    w * field[f0 + r - 1, part, :],
                    w * field[f0 + r + 1, part, :],
                    w * pltpu.roll(c, 1, 1),
                    w * pltpu.roll(c, z.cols - 1, 1),
                    w * c,
                ]
                sums = [x + y for x, y in zip(sums, terms)]
            north, south, west, east, own = [jnp.sum(x, axis=0, keepdims=True) for x in sums]
            west = jnp.where(lane == 0, 0.0, west)
            east = jnp.where(lane == z.cols - 1, 0.0, east)
            rows.append([north - own, south - own, west - own, east - own])
        return rows


def kernel(z, *refs):
    small = ["stencil", "sea", "sites", "data", "prec"]
    names = ["prior", "cot"] + [name + "_in" for name in small] + ["grad", "coef"]
    names += list(scratch_of(z))
    g = Step(z, dict(zip(names, refs)))
    scale = jnp.sqrt(jnp.float32(z.total - 1))
    s, m = g.s_id, g.m_id
    r, ext = z.rows, z.rows + 4
    mine = g.block(m)

    entered = g.barrier()
    loads = []
    for i in range(r):
        loads.append(pltpu.make_async_copy(g.prior.at[:, i], g.pext.at[2 + i], g.own.at[0, i]))
    for i in range(r):
        loads.append(pltpu.make_async_copy(g.cot.at[:, i], g.cotf.at[i, mine], g.own.at[1, i]))
    few = [
        pltpu.make_async_copy(getattr(g, name + "_in"), getattr(g, name), g.few.at[i])
        for i, name in enumerate(small)
    ]
    for copy in loads[:r] + few + loads[r:]:
        copy.start()
    for copy in few:
        copy.wait()
    for i in range(r):
        g.aux[2 + i, 0:4, :] = g.stencil[:, i, :]
        g.aux[2 + i, 4:5, :] = g.sea[i : i + 1, :].astype(F32)
        g.aux[2 + i, 5:6, :] = g.sites[...].astype(F32)
        g.aux[2 + i, 6:8, :] = jnp.zeros((2, z.cols), F32)
    for e, edge in ((0, 0), (1, 0), (ext - 2, z.n_space - 1), (ext - 1, z.n_space - 1)):
        @pl.when(s == edge)
        def _():
            g.pext[e] = jnp.zeros((z.members, z.cols), F32)
            g.mixed[e] = jnp.zeros((z.members, z.cols), F32)
            g.aux[e] = jnp.zeros((8, z.cols), F32)
            g.picked[1 if e < 2 else 2] = jnp.zeros((z.members, z.sites), F32)
    for copy in loads[:r]:
        copy.wait()
    entered()
    halo = g.halo_send(g.pext, g.halo)
    for copy in loads[r:]:
        copy.wait()
    cot_forward, cot_wait = g.pair_gather(lambda which: g.cotf.at[:, g.block(which)], g.cot_sem)
    aux_halo = g.halo_send(g.aux, g.aux_halo)
    g.mark_sites()
    aux_halo()
    g.mark_sites_beside()
    cot_forward()
    halo()

    g.advance(g.pext, 1, g.fext, r + 2)
    g.advance(g.fext, 2, g.state, r)
    g.obsf[m] = g.observe()
    obs_wait = g.mem_send(g.obsf, g.obs_sem)
    own_sums = [jnp.sum(g.state[i], axis=0, keepdims=True) for i in range(r)]
    padding = [jnp.zeros((-r % 8, z.cols), F32)] * (r % 8 > 0)
    g.sums[m] = jnp.concatenate(own_sums + padding, axis=0)
    sums_wait = g.mem_send(g.sums, g.sum_sem)
    cot_wait()
    for i in range(r):
        g.chi[i], g.clo[i] = split(g.cotf[i])
    dev = [split((g.state[i] - own_sums[i] / z.members) / scale) for i in range(r)]
    mean_bar = g.cross_rows(dev)
    sums_wait()
    obs_wait()
    g.pack_gram(scale, mean_bar, own_sums)

    gram, cross = Reduction(g, "gram"), Reduction(g, "cross")
    gram.scatter()
    g.send_lines()
    g.pack_cross()
    cross.scatter()
    gram.start()
    lines_wait = g.sum_lines()
    gram.forward_all()
    cross.start()
    gram.pass_on()
    cross.forward_all()
    lines_wait()
    gram.finish()
    parts = g.transform(scale, gram)
    next(parts)
    cross.pass_on()
    bar_halo = next(parts)
    cross.finish()
    g.picked[0] = g.respond(scale, cross)
    pick_wait = g.between(
        g.picked.at[0], g.picked.at[1], g.picked.at[0], g.picked.at[2], g.pick_sem
    )
    g.spread(0, range(2, r + 2))
    second = g.coefficient_terms(g.sbext, 2, g.fext, 1)
    bar_halo()
    g.pull_back(g.sbext, 1, g.fbar, range(2, r), True)
    pick_wait()
    g.spread(1, (0, 1))
    g.spread(2, (r + 2, r + 3))
    g.pull_back(g.sbext, 1, g.fbar, (0, 1, r, r + 1), True)
    firsts = g.coefficient_terms(g.fbar, 1, g.pext, 2)
    g.cbuf[m] = jnp.concatenate(
        [second[i][k] + firsts[i][k] for k in range(4) for i in range(r)], axis=0
    )
    c_wait = g.mem_send(g.cbuf, g.c_sem)
    g.pull_back(g.fbar, 2, g.grad, range(r), False)
    c_wait()
    both = g.cbuf[0]
    for k in range(1, z.n_mem):
        both = both + g.cbuf[k]
    for k in range(4):
        g.coef[k] = both[k * r : (k + 1) * r]
    g.finish_sends()


def place(z, last, sums, grad, coef, scaled, sem):
    stores = [pltpu.make_async_copy(last.at[i], grad.at[:, i], sem.at[i]) for i in range(z.rows)]
    for copy in stores:
        copy.start()
    scaled[...] = sums[...] / jnp.sqrt(jnp.float32(z.total))
    stores.append(pltpu.make_async_copy(scaled, coef, sem.at[z.rows]))
    stores[-1].start()
    for copy in stores:
        copy.wait()


def local(n_space, n_mem, prior, stencil, sea_mask, sites, data, precision, cotangent):
    z = Sizes(n_space, n_mem, prior, sites)
    any_spec = pl.BlockSpec(memory_space=pl.ANY)
    turned = (z.rows, z.members, z.cols)
    factors = (4, z.rows, z.cols)
    inputs = (prior, cotangent, stencil, sea_mask, sites, data[None], precision[None])
    last, sums = pl.pallas_call(
        functools.partial(kernel, z),
        out_shape=(jax.ShapeDtypeStruct(turned, F32), jax.ShapeDtypeStruct(factors, F32)),
        in_specs=[pl.BlockSpec(memory_space=pltpu.HBM)] * 7,
        out_specs=(VMEM_SPEC, VMEM_SPEC),
        scratch_shapes=list(scratch_of(z).values()),
        compiler_params=pltpu.CompilerParams(
            collective_id=1, has_side_effects=True, vmem_limit_bytes=GRANT
        ),
        name="adjoint",
    )(*[pltpu.with_memory_space_constraint(x, pltpu.HBM) for x in inputs])
    return pl.pallas_call(
        functools.partial(place, z),
        out_shape=(jax.ShapeDtypeStruct(prior.shape, F32), jax.ShapeDtypeStruct(factors, F32)),
        in_specs=[VMEM_SPEC, VMEM_SPEC],
        out_specs=(any_spec, any_spec),
        scratch_shapes=[pltpu.VMEM(factors, F32), pltpu.SemaphoreType.DMA((z.rows + 1,))],
        compiler_params=pltpu.CompilerParams(vmem_limit_bytes=4 * 1024 * 1024),
        name="place",
    )(last, sums)


def solution(mesh):
    placed = (
        P("mem", "space", None),
        P(None, "space", None),
        P("space", None),
        P("space", None),
        P("space"),
        P("space"),
        P("mem", "space", None),
    )
    return jax.shard_map(
        functools.partial(local, mesh.shape["space"], mesh.shape["mem"]),
        mesh=mesh,
        in_specs=placed,
        out_specs=(P("mem", "space", None), P(None, "space", None)),
        check_vma=False,
    )
```

time: 67.3 us -> 57.5 us (0.85)
  Pallas kernels: 62 us -> 56.6 us
  local copies, waits for them, and re-layouts: 4.27 us -> 0 us
    pallas_call x1, Pallas kernels: 62 us -> 55.9 us  [local(): pl.pallas_call(functools.partial(kernel, z), out_shape=(jax.ShapeDtypeStr...]
    unnamed x4 -> x0, local copies, waits for them, and re-layouts: 2.43 us -> none
    transpose x1 -> x0, local copies, waits for them, and re-layouts: 1.84 us -> none  [local(): jnp.transpose(cotangent, (1, 0, 2))]
    pallas_call x0 -> x1, Pallas kernels: none -> 0.74 us  [local(): pl.pallas_call(functools.partial(place, z), out_shape=(jax.ShapeDtypeStru...]
where the time goes in v1:
time: 57.5 us; the launch traced here: 57.3 us
  Pallas kernels  56.6 us (98%)
  between operations  0.64 us (1%)
    pallas_call x1, Pallas kernels, local(): pl.pallas_call(functools.partial(kernel, z), out_shape=(jax.ShapeDtypeStr...  55.9 us

profile of v1, /device:TPU:5, one launch (start us, length us, event | category | flops | bytes accessed | tf_op | source)
XLA Modules:
  0.0 57.3 jit_solution(10818064878083373187)
XLA Ops:
  0.6 55.9 %adjoint.1 = (f32[4,128,128]{2,1,0:T(8,128)S(1)}, f32[4,4,128]{2,1,0:T(4,128)S(1)}) custom-call(f32[128,4,128]{2,1,0:T(4,128)} %refs_0_.1, f32[128,4,128]{2,1,0:T(4,128)} %refs_1_.1, f32[4,4,128]{2,1,0:T(4,128)} %refs_2_.1, s32[4,128]{1,0:T(4,128)} %refs_3_.1, s32[1,128]{1,0:T(1,128)} %refs_4_.1, f32[1,128]{1,0:T(1,128)} %bitcast.2, f32[1,128]{1,0:T(1,128)} %bitcast.3), custom_call_target="tpu_custom_call" | custom-call | tf_op jit(solution)/shard_map/adjoint/pallas_call | solution.py:854
  56.5 0.7 %place.1 = (f32[128,4,128]{2,1,0:T(4,128)}, f32[4,4,128]{2,1,0:T(4,128)}) custom-call(f32[4,128,128]{2,1,0:T(8,128)S(1)} %get-tuple-element.4.last, f32[4,4,128]{2,1,0:T(4,128)S(1)} %get-tuple-element.5.sums), custom_call_target="tpu_custom_call" | custom-call | tf_op jit(solution)/shard_map/place/pallas_call | solution.py:865

commit v2 on v1

--- a/solution.py
+++ b/solution.py
@@ -71,6 +71,7 @@
         self.groups = self.far // self.group
         self.height = n_mem // 2 * self.members // n_space
         self.lines = 8 * pl.cdiv(4 + n_mem, 8)
+        self.rounds = max(0, (n_space - 1).bit_length() - 1)
 
 
 def scratch_of(z):
@@ -88,6 +89,7 @@
         data=v(1, z.sites),
         prec=v(1, z.sites),
         few=dma((5,)),
+        token=pltpu.SemaphoreType.REGULAR((max(1, z.rounds), 2)),
         pext=v(ext, z.members, z.cols),
         aux=v(ext, 8, z.cols),
         cotf=v(z.rows, z.total, z.cols),
@@ -276,8 +278,7 @@
 
     def barrier(self):
         z, s, m = self.z, self.s_id, self.m_id
-        peers = [(lax.rem(s + k, z.n_space), m) for k in range(1, z.n_space)]
-        peers += [(s, lax.rem(m + k, z.n_mem)) for k in range(1, z.n_mem)]
+        peers = [(s, lax.rem(m + k, z.n_mem)) for k in range(1, z.n_mem)]
         a, b = s // z.near, lax.rem(s, z.near)
         p, q = m // z.half, lax.rem(m, z.half)
         for kb in range(1, z.near):
@@ -286,9 +287,37 @@
                     a * z.near + lax.rem(b + kb, z.near), lax.rem(p + kp, z.wide) * z.half + q
                 ))
         barrier = pltpu.get_barrier_semaphore()
+        count = len(peers)
         for peer in peers:
             pl.semaphore_signal(barrier, inc=1, device_id=peer, device_id_type=MESH)
-        return lambda: pl.semaphore_wait(barrier, len(peers))
+        for step in (1, -1, 2, -2):
+            there = self.exists(step)
+            count = count + there.astype(jnp.int32)
+
+            @pl.when(there)
+            def _():
+                pl.semaphore_signal(barrier, inc=1, device_id=(s + step, m), device_id_type=MESH)
+
+        return lambda: pl.semaphore_wait(barrier, count)
+
+    def exists(self, step):
+        to = self.s_id + step
+        return (to >= 0) & (to < self.z.n_space)
+
+    def vouch(self, round_):
+        for side, step in ((0, 2**round_), (1, -(2**round_))):
+            @pl.when(self.exists(step))
+            def _():
+                pl.semaphore_signal(
+                    self.token.at[round_ - 1, side], inc=1,
+                    device_id=(self.s_id + step, self.m_id), device_id_type=MESH,
+                )
+
+    def hear(self, round_):
+        for side, step in ((0, -(2**round_)), (1, 2**round_)):
+            @pl.when(self.exists(step))
+            def _():
+                pl.semaphore_wait(self.token.at[round_ - 1, side], 1)
 
     def between(self, up_src, up_dst, down_src, down_dst, sem):
         z, s, m = self.z, self.s_id, self.m_id
@@ -475,7 +504,7 @@
         self.waits += [(copy, None) for copy in self.d_copies]
         return mean_bar
 
-    def pack_gram(self, scale, mean_bar, own_sums):
+    def pack_gram(self, scale):
         z, m = self.z, self.m_id
         n, size = z.n_mem, z.members
         half = size // 2
@@ -484,8 +513,6 @@
             mean = mean + jnp.sum(self.obsf[k], axis=0, keepdims=True)
         mean = mean / z.total
         prec = self.prec[...]
-        innov = prec * (self.data[...] - mean)
-        self.innov[0:1, :] = innov
         for k in range(n):
             rows = slice(k * size, (k + 1) * size)
             self.ahi[rows, :], self.alo[rows, :] = split((self.obsf[k] - mean) * (prec / scale))
@@ -499,7 +526,14 @@
         for k in range(1, n // 2):
             parts.append(mm3_t(mine, anom(self.block(lax.rem(m + k, n)))))
         self.gram_src[...] = jnp.concatenate(parts, axis=0).reshape(z.n_space, z.height, size)
-
+        return mean, diag
+
+    def pack_lines(self, scale, mean_bar, own_sums, mean, diag):
+        z, m = self.z, self.m_id
+        n, size = z.n_mem, z.members
+        prec = self.prec[...]
+        innov = prec * (self.data[...] - mean)
+        self.innov[0:1, :] = innov
         cross = self.dmat[0]
         self.cross_diag = 0.5 * (cross + cross.T)
         exact = (self.obsf[m] - mean) * (prec / scale)
@@ -762,6 +796,8 @@
         copy.wait()
     entered()
     halo = g.halo_send(g.pext, g.halo)
+    if z.rounds:
+        g.vouch(1)
     for copy in loads[r:]:
         copy.wait()
     cot_forward, cot_wait = g.pair_gather(lambda which: g.cotf.at[:, g.block(which)], g.cot_sem)
@@ -770,6 +806,9 @@
     aux_halo()
     g.mark_sites_beside()
     cot_forward()
+    for k in range(1, z.rounds):
+        g.hear(k)
+        g.vouch(k + 1)
     halo()
 
     g.advance(g.pext, 1, g.fext, r + 2)
@@ -785,12 +824,14 @@
         g.chi[i], g.clo[i] = split(g.cotf[i])
     dev = [split((g.state[i] - own_sums[i] / z.members) / scale) for i in range(r)]
     mean_bar = g.cross_rows(dev)
-    sums_wait()
     obs_wait()
-    g.pack_gram(scale, mean_bar, own_sums)
-
+    mean, diag = g.pack_gram(scale)
+    if z.rounds:
+        g.hear(z.rounds)
     gram, cross = Reduction(g, "gram"), Reduction(g, "cross")
     gram.scatter()
+    sums_wait()
+    g.pack_lines(scale, mean_bar, own_sums, mean, diag)
     g.send_lines()
     g.pack_cross()
     cross.scatter()

time: 57.5 us -> 55.2 us (0.960)
  Pallas kernels: 56.6 us -> 54.4 us
    pallas_call x1, Pallas kernels: 55.9 us -> 53.6 us  [local(): pl.pallas_call(functools.partial(kernel, z), out_shape=(jax.ShapeDtypeStr...]
where the time goes in v2:
time: 55.2 us; the launch traced here: 55 us
  Pallas kernels  54.4 us (99%)
  between operations  0.64 us (1%)
    pallas_call x1, Pallas kernels, local(): pl.pallas_call(functools.partial(kernel, z), out_shape=(jax.ShapeDtypeStr...  53.6 us

profile of v2, /device:TPU:5, one launch (start us, length us, event | category | flops | bytes accessed | tf_op | source)
XLA Modules:
  0.0 55.0 jit_solution(16164241963039679355)
XLA Ops:
  0.6 53.6 %adjoint.1 = (f32[4,128,128]{2,1,0:T(8,128)S(1)}, f32[4,4,128]{2,1,0:T(4,128)S(1)}) custom-call(f32[128,4,128]{2,1,0:T(4,128)} %refs_0_.1, f32[128,4,128]{2,1,0:T(4,128)} %refs_1_.1, f32[4,4,128]{2,1,0:T(4,128)} %refs_2_.1, s32[4,128]{1,0:T(4,128)} %refs_3_.1, s32[1,128]{1,0:T(1,128)} %refs_4_.1, f32[1,128]{1,0:T(1,128)} %bitcast.2, f32[1,128]{1,0:T(1,128)} %bitcast.3), custom_call_target="tpu_custom_call" | custom-call | tf_op jit(solution)/shard_map/adjoint/pallas_call | solution.py:895
  54.3 0.7 %place.1 = (f32[128,4,128]{2,1,0:T(4,128)}, f32[4,4,128]{2,1,0:T(4,128)}) custom-call(f32[4,128,128]{2,1,0:T(8,128)S(1)} %get-tuple-element.4.last, f32[4,4,128]{2,1,0:T(4,128)S(1)} %get-tuple-element.5.sums), custom_call_target="tpu_custom_call" | custom-call | tf_op jit(solution)/shard_map/place/pallas_call | solution.py:906

commit v3 on v2

--- a/solution.py
+++ b/solution.py
@@ -92,17 +92,19 @@
         token=pltpu.SemaphoreType.REGULAR((max(1, z.rounds), 2)),
         pext=v(ext, z.members, z.cols),
         aux=v(ext, 8, z.cols),
-        cotf=v(z.rows, z.total, z.cols),
-        chi=b(z.rows, z.total, z.cols),
-        clo=b(z.rows, z.total, z.cols),
+        cotf=v(ext, z.total, z.cols),
+        chi=b(ext, z.total, z.cols),
+        clo=b(ext, z.total, z.cols),
+        seen=v(z.members, z.sites),
+        beside_seen=v(2, z.n_mem, z.members, z.sites),
+        slope=v(z.members, 3 * z.sites),
         fext=v(z.rows + 2, z.members, z.cols),
         state=v(z.rows, z.members, z.cols),
         hot=b(ext, z.cols, z.sites),
         obsf=v(z.n_mem, z.members, z.sites),
-        tanh=v(z.members, z.sites),
-        ahi=b(z.total, z.sites),
-        alo=b(z.total, z.sites),
-        innov=v(8, z.sites),
+        ahi=b(z.total, 3 * z.sites),
+        alo=b(z.total, 3 * z.sites),
+        innov=v(8, 3 * z.sites),
         sums=v(z.n_mem, 8 * pl.cdiv(z.rows, 8), z.cols),
         dmat=v(z.n_mem, z.members, z.members),
         dx=v(z.n_mem, z.members, z.members),
@@ -122,15 +124,16 @@
         vcol=v(z.total, z.lines),
         sbext=v(ext, z.members, z.cols),
         mixed=v(ext, z.members, z.cols),
-        picked=v(3, z.members, z.sites),
+        picked=v(z.members, 3 * z.sites),
         fbar=v(z.rows + 2, z.members, z.cols),
         cbuf=v(z.n_mem, 4 * z.rows, z.cols),
         own=dma((2, z.rows)),
         halo=dma((2, 2)),
         aux_halo=dma((2, 2)),
         bar_halo=dma((2, 2)),
-        pick_sem=dma((2, 2)),
+        seen_halo=dma((2, 2)),
         cot_sem=dma((2, z.half, z.wide)),
+        seen_sem=dma((2, z.half, z.wide)),
         obs_sem=dma((2, z.n_mem)),
         sum_sem=dma((2, z.n_mem)),
         d_sem=dma((2, z.n_mem)),
@@ -425,9 +428,29 @@
         for r in range(z.rows):
             for piece in split3(self.state[r]):
                 picked = picked + plain(piece, self.hot[2 + r])
+        self.seen[...] = picked
         tanh = jnp.tanh(picked)
-        self.tanh[...] = tanh
+        self.slope[:, : z.sites] = 1.0 + 0.5 * (1.0 - tanh * tanh)
         return picked + 0.5 * tanh
+
+    def observe_beside(self):
+        z = self.z
+        scale = jnp.sqrt(jnp.float32(z.total - 1))
+        for side, e in ((0, 1), (1, z.rows + 2)):
+            cols = slice((1 + side) * z.sites, (2 + side) * z.sites)
+            prec, data = self.aux[e, 6:7, :], self.aux[e, 7:8, :]
+            found, mean = [], jnp.zeros((1, z.sites), F32)
+            for k in range(z.n_mem):
+                picked = self.beside_seen[side, k]
+                found.append(picked + 0.5 * jnp.tanh(picked))
+                mean = mean + jnp.sum(found[-1], axis=0, keepdims=True)
+            mean = mean / z.total
+            for k in range(z.n_mem):
+                rows = slice(k * z.members, (k + 1) * z.members)
+                self.ahi[rows, cols], self.alo[rows, cols] = split((found[k] - mean) * (prec / scale))
+            tanh = jnp.tanh(self.beside_seen[side, self.m_id])
+            self.slope[:, cols] = 1.0 + 0.5 * (1.0 - tanh * tanh)
+            self.innov[0:1, cols] = prec * (data - mean)
 
     def mark(self, e, row, sites):
         z = self.z
@@ -446,7 +469,8 @@
             self.mark(r + 2 + k, k, high)
 
     def spread(self, slot, rows):
-        hi, lo = split(self.picked[slot])
+        z = self.z
+        hi, lo = split(self.picked[:, slot * z.sites : (slot + 1) * z.sites])
         for e in rows:
             field = self.mixed[e] + plain_t(hi, self.hot[e]) + plain_t(lo, self.hot[e])
             self.sbext[e] = self.aux[e, 4:5, :] * field
@@ -480,9 +504,9 @@
         for k in list(range(n - 1, 0, -1)) + [0]:
             there = lax.rem(m + k, n)
             rows = self.block(there)
-            part = mm3_t(dev[0], (self.chi[0, rows, :], self.clo[0, rows, :]))
+            part = mm3_t(dev[0], (self.chi[2, rows, :], self.clo[2, rows, :]))
             for i in range(1, z.rows):
-                part = part + mm3_t(dev[i], (self.chi[i, rows, :], self.clo[i, rows, :]))
+                part = part + mm3_t(dev[i], (self.chi[2 + i, rows, :], self.clo[2 + i, rows, :]))
             mean_bar = mean_bar + jnp.sum(part, axis=1, keepdims=True)
             if 2 * k == n:
                 part = jnp.where(self.hi == 0, part, part.T)
@@ -515,8 +539,8 @@
         prec = self.prec[...]
         for k in range(n):
             rows = slice(k * size, (k + 1) * size)
-            self.ahi[rows, :], self.alo[rows, :] = split((self.obsf[k] - mean) * (prec / scale))
-        anom = lambda rows: (self.ahi[rows, :], self.alo[rows, :])
+            self.ahi[rows, : z.sites], self.alo[rows, : z.sites] = split((self.obsf[k] - mean) * (prec / scale))
+        anom = lambda rows: (self.ahi[rows, : z.sites], self.alo[rows, : z.sites])
         mine = anom(self.block(m))
         diag = mm3_t(mine, mine)
         parts = [self.fold(diag)]
@@ -533,7 +557,7 @@
         n, size = z.n_mem, z.members
         prec = self.prec[...]
         innov = prec * (self.data[...] - mean)
-        self.innov[0:1, :] = innov
+        self.innov[0:1, : z.sites] = innov
         cross = self.dmat[0]
         self.cross_diag = 0.5 * (cross + cross.T)
         exact = (self.obsf[m] - mean) * (prec / scale)
@@ -550,7 +574,7 @@
         term = None
         for r in range(z.rows):
             lacks = (own_sums[r] / size - total[r : r + 1] / z.total) / scale
-            this = mm3_t(split(jnp.broadcast_to(lacks, (8, z.cols))), (self.chi[r], self.clo[r]))
+            this = mm3_t(split(jnp.broadcast_to(lacks, (8, z.cols))), (self.chi[2 + r], self.clo[2 + r]))
             term = this if term is None else term + this
         lines = [stacked.T[:4]] + [term[:1, k * size : (k + 1) * size] for k in range(n)]
         if z.lines > 4 + n:
@@ -652,8 +676,8 @@
         mix = self.s[mine, :] / root + self.vcol[mine, 0:1] / scale
         row_weights = self.first[3:4] + jnp.sum(second[0:1], axis=1, keepdims=True) / scale
         mix = split(mix + (1.0 - row_weights) / total)
-        for r in range(z.rows):
-            self.mixed[2 + r] = mm3(mix, (self.chi[r], self.clo[r]))
+        for e in range(2, z.rows + 2):
+            self.mixed[e] = mm3(mix, (self.chi[e], self.clo[e]))
         bar_halo = self.halo_send(self.mixed, self.bar_halo)
         self.fg[...] = mm3((self.fh[...], self.fl[...]), g_split)
         self.weigh[...] = 2.25 * identity + 4.5 * (self.fg[...] + self.f[...] - self.s[...])
@@ -701,11 +725,11 @@
         ).astype(F32) - 1.0 / total
         sym = 2.0 * scale_bar * (3.0 * unit - 2.0 * self.centred(self.f)) - bar / norm
         sym = sym - (scale / total) * self.pull_bar
-        observed = (self.prec[...] / scale) * (
+        prec = [self.prec[...], self.aux[1, 6:7, :], self.aux[z.rows + 2, 6:7, :]]
+        observed = (jnp.concatenate(prec, axis=1) / scale) * (
             mm3(split(sym), (self.ahi[...], self.alo[...])) + self.pull_mine * self.innov[0:1, :]
         )
-        tanh = self.tanh[...]
-        return observed * (1.0 + 0.5 * (1.0 - tanh * tanh))
+        return observed * self.slope[...]
 
 
     def pull_back(self, src, first, dst, rows, to_sea):
@@ -771,7 +795,7 @@
     for i in range(r):
         loads.append(pltpu.make_async_copy(g.prior.at[:, i], g.pext.at[2 + i], g.own.at[0, i]))
     for i in range(r):
-        loads.append(pltpu.make_async_copy(g.cot.at[:, i], g.cotf.at[i, mine], g.own.at[1, i]))
+        loads.append(pltpu.make_async_copy(g.cot.at[:, i], g.cotf.at[2 + i, mine], g.own.at[1, i]))
     few = [
         pltpu.make_async_copy(getattr(g, name + "_in"), getattr(g, name), g.few.at[i])
         for i, name in enumerate(small)
@@ -784,14 +808,15 @@
         g.aux[2 + i, 0:4, :] = g.stencil[:, i, :]
         g.aux[2 + i, 4:5, :] = g.sea[i : i + 1, :].astype(F32)
         g.aux[2 + i, 5:6, :] = g.sites[...].astype(F32)
-        g.aux[2 + i, 6:8, :] = jnp.zeros((2, z.cols), F32)
+        g.aux[2 + i, 6:7, :] = g.prec[...]
+        g.aux[2 + i, 7:8, :] = g.data[...]
     for e, edge in ((0, 0), (1, 0), (ext - 2, z.n_space - 1), (ext - 1, z.n_space - 1)):
         @pl.when(s == edge)
         def _():
             g.pext[e] = jnp.zeros((z.members, z.cols), F32)
             g.mixed[e] = jnp.zeros((z.members, z.cols), F32)
             g.aux[e] = jnp.zeros((8, z.cols), F32)
-            g.picked[1 if e < 2 else 2] = jnp.zeros((z.members, z.sites), F32)
+            g.beside_seen[0 if e < 2 else 1, m] = jnp.zeros((z.members, z.sites), F32)
     for copy in loads[:r]:
         copy.wait()
     entered()
@@ -800,7 +825,7 @@
         g.vouch(1)
     for copy in loads[r:]:
         copy.wait()
-    cot_forward, cot_wait = g.pair_gather(lambda which: g.cotf.at[:, g.block(which)], g.cot_sem)
+    cot_forward, cot_wait = g.pair_gather(lambda which: g.cotf.at[pl.ds(2, r), g.block(which)], g.cot_sem)
     aux_halo = g.halo_send(g.aux, g.aux_halo)
     g.mark_sites()
     aux_halo()
@@ -819,9 +844,12 @@
     padding = [jnp.zeros((-r % 8, z.cols), F32)] * (r % 8 > 0)
     g.sums[m] = jnp.concatenate(own_sums + padding, axis=0)
     sums_wait = g.mem_send(g.sums, g.sum_sem)
+    seen_halo = g.between(
+        g.seen, g.beside_seen.at[0, m], g.seen, g.beside_seen.at[1, m], g.seen_halo
+    )
     cot_wait()
-    for i in range(r):
-        g.chi[i], g.clo[i] = split(g.cotf[i])
+    for e in range(2, r + 2):
+        g.chi[e], g.clo[e] = split(g.cotf[e])
     dev = [split((g.state[i] - own_sums[i] / z.members) / scale) for i in range(r)]
     mean_bar = g.cross_rows(dev)
     obs_wait()
@@ -835,10 +863,19 @@
     g.send_lines()
     g.pack_cross()
     cross.scatter()
+    seen_halo()
+    extras = [
+        g.pair_gather(lambda which: g.beside_seen.at[:, which], g.seen_sem),
+    ]
     gram.start()
     lines_wait = g.sum_lines()
+    for forward, _ in extras:
+        forward()
     gram.forward_all()
     cross.start()
+    for _, wait in extras:
+        wait()
+    g.observe_beside()
     gram.pass_on()
     cross.forward_all()
     lines_wait()
@@ -848,15 +885,11 @@
     cross.pass_on()
     bar_halo = next(parts)
     cross.finish()
-    g.picked[0] = g.respond(scale, cross)
-    pick_wait = g.between(
-        g.picked.at[0], g.picked.at[1], g.picked.at[0], g.picked.at[2], g.pick_sem
-    )
+    g.picked[...] = g.respond(scale, cross)
     g.spread(0, range(2, r + 2))
     second = g.coefficient_terms(g.sbext, 2, g.fext, 1)
+    g.pull_back(g.sbext, 1, g.fbar, range(2, r), True)
     bar_halo()
-    g.pull_back(g.sbext, 1, g.fbar, range(2, r), True)
-    pick_wait()
     g.spread(1, (0, 1))
     g.spread(2, (r + 2, r + 3))
     g.pull_back(g.sbext, 1, g.fbar, (0, 1, r, r + 1), True)

time: 55.2 us -> 52.4 us (0.949)
  Pallas kernels: 54.4 us -> 51.6 us
    pallas_call x1, Pallas kernels: 53.6 us -> 50.9 us  [local(): pl.pallas_call(functools.partial(kernel, z), out_shape=(jax.ShapeDtypeStr...]
where the time goes in v3:
time: 52.4 us; the launch traced here: 52.3 us
  Pallas kernels  51.6 us (98%)
  between operations  0.64 us (1%)
    pallas_call x1, Pallas kernels, local(): pl.pallas_call(functools.partial(kernel, z), out_shape=(jax.ShapeDtypeStr...  50.9 us

profile of v3, /device:TPU:5, one launch (start us, length us, event | category | flops | bytes accessed | tf_op | source)
XLA Modules:
  0.0 52.3 jit_solution(4983821367996714139)
XLA Ops:
  0.6 50.9 %adjoint.1 = (f32[4,128,128]{2,1,0:T(8,128)S(1)}, f32[4,4,128]{2,1,0:T(4,128)S(1)}) custom-call(f32[128,4,128]{2,1,0:T(4,128)} %refs_0_.1, f32[128,4,128]{2,1,0:T(4,128)} %refs_1_.1, f32[4,4,128]{2,1,0:T(4,128)} %refs_2_.1, s32[4,128]{1,0:T(4,128)} %refs_3_.1, s32[1,128]{1,0:T(1,128)} %refs_4_.1, f32[1,128]{1,0:T(1,128)} %bitcast.2, f32[1,128]{1,0:T(1,128)} %bitcast.3), custom_call_target="tpu_custom_call" | custom-call | tf_op jit(solution)/shard_map/adjoint/pallas_call | solution.py:928
  51.5 0.7 %place.1 = (f32[128,4,128]{2,1,0:T(4,128)}, f32[4,4,128]{2,1,0:T(4,128)}) custom-call(f32[4,128,128]{2,1,0:T(8,128)S(1)} %get-tuple-element.4.last, f32[4,4,128]{2,1,0:T(4,128)S(1)} %get-tuple-element.5.sums), custom_call_target="tpu_custom_call" | custom-call | tf_op jit(solution)/shard_map/place/pallas_call | solution.py:939

commit v4 on v3

--- a/solution.py
+++ b/solution.py
@@ -131,6 +131,7 @@
         halo=dma((2, 2)),
         aux_halo=dma((2, 2)),
         bar_halo=dma((2, 2)),
+        far_halo=dma((2, 2)),
         seen_halo=dma((2, 2)),
         cot_sem=dma((2, z.half, z.wide)),
         seen_sem=dma((2, z.half, z.wide)),
@@ -558,8 +559,6 @@
         prec = self.prec[...]
         innov = prec * (self.data[...] - mean)
         self.innov[0:1, : z.sites] = innov
-        cross = self.dmat[0]
-        self.cross_diag = 0.5 * (cross + cross.T)
         exact = (self.obsf[m] - mean) * (prec / scale)
         lane = lax.broadcasted_iota(jnp.int32, (size, size), 1)
         diagonal = lambda x: jnp.sum(jnp.where(eye(size), x, 0.0), axis=1, keepdims=True)
@@ -587,6 +586,8 @@
         half = size // 2
         for copy in self.d_copies:
             copy.wait_recv()
+        cross = self.dmat[0]
+        self.cross_diag = 0.5 * (cross + cross.T)
         parts = [self.fold(self.cross_diag)]
         ours = pl.ds(pl.multiple_of(self.hi * half, half), half)
         parts.append(0.5 * (self.dmat[n // 2, ours] + self.dx[n // 2, pl.ds(0, half)]))
@@ -678,7 +679,12 @@
         mix = split(mix + (1.0 - row_weights) / total)
         for e in range(2, z.rows + 2):
             self.mixed[e] = mm3(mix, (self.chi[e], self.clo[e]))
-        bar_halo = self.halo_send(self.mixed, self.bar_halo)
+        r = z.rows
+        row = lambda e: self.mixed.at[e]
+        bar_halo = (
+            self.between(row(r + 1), row(1), row(2), row(r + 2), self.bar_halo),
+            self.between(row(r), row(0), row(3), row(r + 3), self.far_halo),
+        )
         self.fg[...] = mm3((self.fh[...], self.fl[...]), g_split)
         self.weigh[...] = 2.25 * identity + 4.5 * (self.fg[...] + self.f[...] - self.s[...])
         self.norm, self.root = norm, root
@@ -756,11 +762,11 @@
                     + west * pltpu.roll(v, 1, 1)
                 )
 
-    def coefficient_terms(self, weight, w0, field, f0):
+    def coefficient_terms(self, weight, w0, field, f0, which):
         z = self.z
         lane = lax.broadcasted_iota(jnp.int32, (1, z.cols), 1)
-        rows = []
-        for r in range(z.rows):
+        rows = {}
+        for r in which:
             sums = [0.0] * 5
             for part in self.chunks():
                 w = weight[w0 + r, part, :]
@@ -776,7 +782,7 @@
             north, south, west, east, own = [jnp.sum(x, axis=0, keepdims=True) for x in sums]
             west = jnp.where(lane == 0, 0.0, west)
             east = jnp.where(lane == z.cols - 1, 0.0, east)
-            rows.append([north - own, south - own, west - own, east - own])
+            rows[r] = [north - own, south - own, west - own, east - own]
         return rows
 
 
@@ -858,26 +864,26 @@
         g.hear(z.rounds)
     gram, cross = Reduction(g, "gram"), Reduction(g, "cross")
     gram.scatter()
+    g.pack_cross()
+    cross.scatter()
     sums_wait()
     g.pack_lines(scale, mean_bar, own_sums, mean, diag)
     g.send_lines()
-    g.pack_cross()
-    cross.scatter()
     seen_halo()
     extras = [
         g.pair_gather(lambda which: g.beside_seen.at[:, which], g.seen_sem),
     ]
     gram.start()
+    cross.start()
     lines_wait = g.sum_lines()
     for forward, _ in extras:
         forward()
     gram.forward_all()
-    cross.start()
+    cross.forward_all()
     for _, wait in extras:
         wait()
     g.observe_beside()
     gram.pass_on()
-    cross.forward_all()
     lines_wait()
     gram.finish()
     parts = g.transform(scale, gram)
@@ -887,17 +893,23 @@
     cross.finish()
     g.picked[...] = g.respond(scale, cross)
     g.spread(0, range(2, r + 2))
-    second = g.coefficient_terms(g.sbext, 2, g.fext, 1)
+    second = g.coefficient_terms(g.sbext, 2, g.fext, 1, range(r))
     g.pull_back(g.sbext, 1, g.fbar, range(2, r), True)
-    bar_halo()
-    g.spread(1, (0, 1))
-    g.spread(2, (r + 2, r + 3))
-    g.pull_back(g.sbext, 1, g.fbar, (0, 1, r, r + 1), True)
-    firsts = g.coefficient_terms(g.fbar, 1, g.pext, 2)
+    firsts = g.coefficient_terms(g.fbar, 1, g.pext, 2, range(1, r - 1))
+    bar_halo[0]()
+    g.spread(1, (1,))
+    g.spread(2, (r + 2,))
+    outer = (0, r - 1) if r > 1 else (0,)
+    g.pull_back(g.sbext, 1, g.fbar, [i + 1 for i in outer], True)
+    firsts.update(g.coefficient_terms(g.fbar, 1, g.pext, 2, outer))
     g.cbuf[m] = jnp.concatenate(
         [second[i][k] + firsts[i][k] for k in range(4) for i in range(r)], axis=0
     )
     c_wait = g.mem_send(g.cbuf, g.c_sem)
+    bar_halo[1]()
+    g.spread(1, (0,))
+    g.spread(2, (r + 3,))
+    g.pull_back(g.sbext, 1, g.fbar, (0, r + 1), True)
     g.pull_back(g.fbar, 2, g.grad, range(r), False)
     c_wait()
     both = g.cbuf[0]

time: 52.4 us -> 51.8 us (0.989)
  Pallas kernels: 51.6 us -> 50.7 us
    pallas_call x1, Pallas kernels: 50.9 us -> 50 us  [local(): pl.pallas_call(functools.partial(kernel, z), out_shape=(jax.ShapeDtypeStr...]
where the time goes in v4:
time: 51.8 us; the launch traced here: 51.4 us
  Pallas kernels  50.7 us (98%)
  between operations  0.64 us (1%)
    pallas_call x1, Pallas kernels, local(): pl.pallas_call(functools.partial(kernel, z), out_shape=(jax.ShapeDtypeStr...  50 us

profile of v4, /device:TPU:5, one launch (start us, length us, event | category | flops | bytes accessed | tf_op | source)
XLA Modules:
  0.0 51.4 jit_solution(90996462180064243)
XLA Ops:
  0.6 50.0 %adjoint.1 = (f32[4,128,128]{2,1,0:T(8,128)S(1)}, f32[4,4,128]{2,1,0:T(4,128)S(1)}) custom-call(f32[128,4,128]{2,1,0:T(4,128)} %refs_0_.1, f32[128,4,128]{2,1,0:T(4,128)} %refs_1_.1, f32[4,4,128]{2,1,0:T(4,128)} %refs_2_.1, s32[4,128]{1,0:T(4,128)} %refs_3_.1, s32[1,128]{1,0:T(1,128)} %refs_4_.1, f32[1,128]{1,0:T(1,128)} %bitcast.2, f32[1,128]{1,0:T(1,128)} %bitcast.3), custom_call_target="tpu_custom_call" | custom-call | tf_op jit(solution)/shard_map/adjoint/pallas_call | solution.py:940
  50.6 0.7 %place.1 = (f32[128,4,128]{2,1,0:T(4,128)}, f32[4,4,128]{2,1,0:T(4,128)}) custom-call(f32[4,128,128]{2,1,0:T(8,128)S(1)} %get-tuple-element.4.last, f32[4,4,128]{2,1,0:T(4,128)S(1)} %get-tuple-element.5.sums), custom_call_target="tpu_custom_call" | custom-call | tf_op jit(solution)/shard_map/place/pallas_call | solution.py:951

commit v5 on v4

--- a/solution.py
+++ b/solution.py
@@ -40,11 +40,13 @@
 
 
 def mm3(a, b):
-    return plain(a[0], b[0]) + (plain(a[0], b[1]) + plain(a[1], b[0]))
+    left = jnp.concatenate([a[0], a[0], a[1]], axis=1)
+    return plain(left, jnp.concatenate([b[0], b[1], b[0]], axis=0))
 
 
 def mm3_t(a, b):
-    return plain_t(a[0], b[0]) + (plain_t(a[0], b[1]) + plain_t(a[1], b[0]))
+    left = jnp.concatenate([a[0], a[0], a[1]], axis=1)
+    return plain_t(left, jnp.concatenate([b[0], b[1], b[0]], axis=1))
 
 
 def whole_sum(x):

time: 51.8 us -> 50.2 us (0.969)
  Pallas kernels: 50.7 us -> 49.2 us
    pallas_call x1, Pallas kernels: 50 us -> 48.4 us  [local(): pl.pallas_call(functools.partial(kernel, z), out_shape=(jax.ShapeDtypeStr...]
where the time goes in v5:
time: 50.2 us; the launch traced here: 49.8 us
  Pallas kernels  49.2 us (98%)
  between operations  0.64 us (1%)
    pallas_call x1, Pallas kernels, local(): pl.pallas_call(functools.partial(kernel, z), out_shape=(jax.ShapeDtypeStr...  48.4 us

profile of v5, /device:TPU:5, one launch (start us, length us, event | category | flops | bytes accessed | tf_op | source)
XLA Modules:
  0.0 49.8 jit_solution(15123331413505840954)
XLA Ops:
  0.6 48.4 %adjoint.1 = (f32[4,128,128]{2,1,0:T(8,128)S(1)}, f32[4,4,128]{2,1,0:T(4,128)S(1)}) custom-call(f32[128,4,128]{2,1,0:T(4,128)} %refs_0_.1, f32[128,4,128]{2,1,0:T(4,128)} %refs_1_.1, f32[4,4,128]{2,1,0:T(4,128)} %refs_2_.1, s32[4,128]{1,0:T(4,128)} %refs_3_.1, s32[1,128]{1,0:T(1,128)} %refs_4_.1, f32[1,128]{1,0:T(1,128)} %bitcast.2, f32[1,128]{1,0:T(1,128)} %bitcast.3), custom_call_target="tpu_custom_call" | custom-call | tf_op jit(solution)/shard_map/adjoint/pallas_call | solution.py:942
  49.1 0.7 %place.1 = (f32[128,4,128]{2,1,0:T(4,128)}, f32[4,4,128]{2,1,0:T(4,128)}) custom-call(f32[4,128,128]{2,1,0:T(8,128)S(1)} %get-tuple-element.4.last, f32[4,4,128]{2,1,0:T(4,128)S(1)} %get-tuple-element.5.sums), custom_call_target="tpu_custom_call" | custom-call | tf_op jit(solution)/shard_map/place/pallas_call | solution.py:953

commit v6 on v5

--- a/solution.py
+++ b/solution.py
@@ -427,10 +427,10 @@
 
     def observe(self):
         z = self.z
-        picked = jnp.zeros((z.members, z.sites), F32)
-        for r in range(z.rows):
-            for piece in split3(self.state[r]):
-                picked = picked + plain(piece, self.hot[2 + r])
+        pieces = [split3(self.state[r]) for r in range(z.rows)]
+        left = jnp.concatenate([pieces[r][k] for k in range(3) for r in range(z.rows)], axis=1)
+        hot = jnp.concatenate([self.hot[2 + r] for r in range(z.rows)] * 3, axis=0)
+        picked = plain(left, hot)
         self.seen[...] = picked
         tanh = jnp.tanh(picked)
         self.slope[:, : z.sites] = 1.0 + 0.5 * (1.0 - tanh * tanh)
@@ -475,7 +475,8 @@
         z = self.z
         hi, lo = split(self.picked[:, slot * z.sites : (slot + 1) * z.sites])
         for e in rows:
-            field = self.mixed[e] + plain_t(hi, self.hot[e]) + plain_t(lo, self.hot[e])
+            hot = jnp.concatenate([self.hot[e], self.hot[e]], axis=1)
+            field = self.mixed[e] + plain_t(jnp.concatenate([hi, lo], axis=1), hot)
             self.sbext[e] = self.aux[e, 4:5, :] * field
 
 
@@ -507,9 +508,13 @@
         for k in list(range(n - 1, 0, -1)) + [0]:
             there = lax.rem(m + k, n)
             rows = self.block(there)
-            part = mm3_t(dev[0], (self.chi[2, rows, :], self.clo[2, rows, :]))
-            for i in range(1, z.rows):
-                part = part + mm3_t(dev[i], (self.chi[2 + i, rows, :], self.clo[2 + i, rows, :]))
+            part = mm3_t(
+                [jnp.concatenate([d[p] for d in dev], axis=1) for p in range(2)],
+                [
+                    jnp.concatenate([ref[2 + i, rows, :] for i in range(z.rows)], axis=1)
+                    for ref in (self.chi, self.clo)
+                ],
+            )
             mean_bar = mean_bar + jnp.sum(part, axis=1, keepdims=True)
             if 2 * k == n:
                 part = jnp.where(self.hi == 0, part, part.T)
@@ -724,9 +729,15 @@
         f_split = (self.fh[...], self.fl[...])
         through = mm3((self.lh[...], self.ll[...]), s_split)
         bar = 1.5 * s_mine + through[2 * size :]
-        bar = bar + mm3(split(mm3(split(s_mine), f_split)), (self.gh[...], self.gl[...]))
-        bar = bar + mm3(split(through[:size]), (self.f2h[...], self.f2l[...]))
-        bar = bar + mm3(split(through[size : 2 * size]), f_split)
+        lefts = [
+            split(mm3(split(s_mine), f_split)), split(through[:size]),
+            split(through[size : 2 * size]),
+        ]
+        rights = [(self.gh, self.gl), (self.f2h, self.f2l), (self.fh, self.fl)]
+        bar = bar + mm3(
+            [jnp.concatenate([x[p] for x in lefts], axis=1) for p in range(2)],
+            [jnp.concatenate([x[p][...] for x in rights], axis=0) for p in range(2)],
+        )
         unit = (
             lax.broadcasted_iota(jnp.int32, (size, total), 0) + m * size
             == lax.broadcasted_iota(jnp.int32, (size, total), 1)

time: 50.2 us -> 50.2 us (level)
  no operation moved by 1% of the time
where the time goes in v6:
time: 50.2 us; the launch traced here: 49.8 us
  Pallas kernels  49.2 us (98%)
  between operations  0.64 us (1%)
    pallas_call x1, Pallas kernels, local(): pl.pallas_call(functools.partial(kernel, z), out_shape=(jax.ShapeDtypeStr...  48.4 us

profile of v6, /device:TPU:5, one launch (start us, length us, event | category | flops | bytes accessed | tf_op | source)
XLA Modules:
  0.0 49.8 jit_solution(14251660895779988193)
XLA Ops:
  0.6 48.4 %adjoint.1 = (f32[4,128,128]{2,1,0:T(8,128)S(1)}, f32[4,4,128]{2,1,0:T(4,128)S(1)}) custom-call(f32[128,4,128]{2,1,0:T(4,128)} %refs_0_.1, f32[128,4,128]{2,1,0:T(4,128)} %refs_1_.1, f32[4,4,128]{2,1,0:T(4,128)} %refs_2_.1, s32[4,128]{1,0:T(4,128)} %refs_3_.1, s32[1,128]{1,0:T(1,128)} %refs_4_.1, f32[1,128]{1,0:T(1,128)} %bitcast.2, f32[1,128]{1,0:T(1,128)} %bitcast.3), custom_call_target="tpu_custom_call" | custom-call | tf_op jit(solution)/shard_map/adjoint/pallas_call | solution.py:953
  49.1 0.7 %place.1 = (f32[128,4,128]{2,1,0:T(4,128)}, f32[4,4,128]{2,1,0:T(4,128)}) custom-call(f32[4,128,128]{2,1,0:T(8,128)S(1)} %get-tuple-element.4.last, f32[4,4,128]{2,1,0:T(4,128)S(1)} %get-tuple-element.5.sums), custom_call_target="tpu_custom_call" | custom-call | tf_op jit(solution)/shard_map/place/pallas_call | solution.py:964
